TPU v7x, 256 devices: a whole 4x4x8 slice. The times are simulated.
256 devices in a mesh: tm: 8 (over y, core), space: 32 (over x, z).
Axes of the slice: x: 4, y: 4, z: 8, core: 2. Of those that a mesh axis runs over, the one named last changes fastest.
Arguments:
- snapshots: float32 [2048, 128, 1024], P('space', None, 'tm'), may hold values from -6 to 6
- land_mask: int32 [2048, 128], P('space'), may hold values 0 or 1
- taps_rows: float32 [6], replicated, may hold values from -2.5 to 2.5
- taps_cols: float32 [6], replicated, may hold values from -2.5 to 2.5
- probes: float32 [1024, 64, 128], P('space'), may hold values from -6 to 6
Outputs:
- basis: float32 [1024, 64, 128], P('space', None, 'tm')
- coefficients: float32 [128, 128], P('tm')
All inputs are finite; a program needn't handle non-finite values. No bound on the sum of `land_mask` on one device may be relied on, other than what follows from the above.
Results may differ from a plain program's by a relative error of at most 0.00028.
Values sent between devices are 32-bit elements; how exact they have to be, the bound alone decides.
A program may use at most 64 MiB of HBM per device.

v0:
```python
import jax
import jax.numpy as jnp
from jax import lax
from jax.sharding import PartitionSpec as P

SIGN_STEPS = 8


exact_dot = lax.Precision.HIGHEST


def padded_2(x, sides, width):
    for axis, dim in sides:
        size, length = (lax.axis_size(axis), x.shape[dim])
        up = [(i, (i + 1) % size) for i in range(size - 1)]
        down = [(j, i) for i, j in up]
        last = lax.slice_in_dim(x, length - width, length, axis=dim)
        initial = lax.slice_in_dim(x, 0, width, axis=dim)
        before = lax.ppermute(last, axis, up)
        after = lax.ppermute(initial, axis, down)
        x = jnp.concatenate([before, x, after], axis=dim)
    return x


def partner(block, axis, distance):
    count = lax.axis_size(axis)
    route = []
    for low in range(count):
        high = low | 1 << distance
        if high != low and high < count:
            route += [(low, high), (high, low)]
    return lax.ppermute(block, axis, route)


def band_matrix(tap_values, out_count, in_width, shift_by):
    row_ids = lax.broadcasted_iota(jnp.int32, (out_count, in_width), 0)
    col_ids = lax.broadcasted_iota(jnp.int32, (out_count, in_width), 1)
    tap_offset = col_ids - 2 * row_ids - shift_by
    band_table = jnp.zeros((out_count, in_width), jnp.float32)
    for tap_index in range(6):
        band_table = band_table + jnp.where(tap_offset == tap_index, tap_values[tap_index], 0.0)
    return band_table


def merge_level(paired):
    partial_gram = jnp.einsum("gra,grb->gab", paired, paired, precision=exact_dot)
    gram_total = lax.psum(partial_gram, "space")
    order_size = gram_total.shape[-1]
    identity = jnp.eye(order_size, dtype=jnp.float32)
    mean_eig = jnp.sum(gram_total * identity, axis=(1, 2)) / order_size
    shifted = gram_total - mean_eig[:, None, None] * identity
    norm_scale = jnp.sqrt(jnp.sum(shifted * shifted, axis=(1, 2)) + 1e-06)
    sign_iter = shifted / norm_scale[:, None, None]
    for sweep_index in range(SIGN_STEPS):
        square = jnp.einsum("gab,gbc->gac", sign_iter, sign_iter, precision=exact_dot)
        sign_iter = 1.5 * sign_iter - 0.5 * jnp.einsum(
            "gab,gbc->gac", sign_iter, square, precision=exact_dot
        )
    projector = 0.5 * (identity + sign_iter)
    half_order = order_size // 2
    combine = projector[:, :, :half_order] + projector[:, :, half_order:]
    return jnp.einsum("gra,gab->grb", paired, combine, precision=exact_dot)


def local(snapshots, land_mask, taps_rows, taps_cols, probes):
    rows_dev, cell_cols, columns = snapshots.shape
    ocean_field = snapshots * land_mask.astype(jnp.float32)[:, :, None]
    across = band_matrix(taps_cols, cell_cols // 2, cell_cols, -2)
    narrowed = jnp.einsum("jy,xys->xjs", across, ocean_field, precision=exact_dot)
    padded = padded_2(narrowed, (("space", 0),), 3)
    row_filter = band_matrix(taps_rows, rows_dev // 2, rows_dev + 6, 1)
    filtered = jnp.einsum("ip,pjs->ijs", row_filter, padded, precision=exact_dot)
    cell_rows = rows_dev // 2 * (cell_cols // 2)
    factor = filtered.reshape(cell_rows, columns)
    flat_probes = probes.reshape(cell_rows, probes.shape[2])
    levels = lax.axis_size("tm").bit_length() - 1
    position = lax.axis_index("tm")
    merged = factor
    for level_index in range(levels):
        partner_fac = partner(merged, "tm", level_index)
        is_upper = position >> level_index & 1 == 1
        lower_part = jnp.where(is_upper, partner_fac, merged)
        upper_part = jnp.where(is_upper, merged, partner_fac)
        merged = merge_level(jnp.concatenate([lower_part, upper_part], axis=1)[None])[0]
    width_dev = columns // lax.axis_size("tm")
    col_start = position * width_dev
    partial_coef = jnp.einsum("rs,rp->sp", merged, flat_probes, precision=exact_dot)
    coefficients = lax.psum(partial_coef, "space")
    basis_own = lax.dynamic_slice_in_dim(merged, col_start, width_dev, 1)
    coef_own = lax.dynamic_slice_in_dim(coefficients, col_start, width_dev, 0)
    return (basis_own.reshape(rows_dev // 2, cell_cols // 2, width_dev), coef_own)


def solution(mesh):
    placed = (P("space", None, "tm"), P("space", None), P(), P(), P("space", None, None))
    return jax.shard_map(
        local,
        mesh=mesh,
        in_specs=placed,
        out_specs=(P("space", None, "tm"), P("tm", None)),
        check_vma=False,
    )
```

profile of v0, /device:TPU:1, one launch (start us, length us, event | category | flops | bytes accessed | tf_op | source)
XLA Modules:
  0.0 720.3 jit_solution(15306966266729676532)
XLA Ops:
  7.2 1.5 fusion.267
  9.5 9.0 %fusion.11 = f32[64,64,128]{2,1,0:T(8,128)S(1)} fusion(f32[64,128,128]{2,1,0:T(8,128)} %param.5, f32[64,128]{1,0:T(8,128)S(1)} %convert_element_type.22, f32[]{:T(128)} %bitcast.12, f32[]{:T(128)} %bitcast.11, f32[]{:T(128)} %bitcast.10, f32[]{:T(128)} %bitcast.9, f32[]{:T(128)} %bitcast.8, f32[]{:T(128)} %bitcast.7, s32[64]{0:T(128)S(1)} %iota_multiply_fusion), kind=kOutput, calls=%fused_computation.15 | convolution fusion | flops 806510592 | bytes 6324504 | tf_op jit(solution)/shard_map/jy,xys->xjs/dot_general | solution.py:69
  18.6 4.4 collective-permute-start
  25.0 3.6 collective-permute-done.1
  28.8 6.5 fusion.2
  35.9 2.0 collective-permute-start.2
  37.9 2.4 collective-permute-done.2
  40.3 1.7 broadcast_select_fusion.1
  42.0 4.2 fusion.14
  46.4 143.6 %all-reduce.5.cloned.1.call-done = f32[1,256,256]{2,1,0:T(8,128)} async-done(((f32[1,256,256]{2,1,0:T(8,128)}), f32[1,256,256]{2,1,0:T(8,128)}) %all-reduce.5.cloned.1.call-update) | async-done | bytes 262160 | tf_op jit(solution)/shard_map/psum | solution.py:47
  190.0 1.6 select_reduce_fusion.2
  192.3 1.6 multiply_reduce_fusion.2
  194.6 1.4 fusion.141
  202.9 3.3 fusion.9
  207.4 18.7 %collective-permute-done.3 = f32[2048,128]{0,1:T(8,128)} collective-permute-done((f32[2048,128]{0,1:T(8,128)}, f32[2048,128]{0,1:T(8,128)}, u32[]{:S(2)}, u32[]{:S(2)}) %collective-permute-start.3) | collective-permute-done | bytes 1048608 | tf_op jit(solution)/shard_map/ppermute | solution.py:32
  226.2 1.7 broadcast_select_fusion.3
  227.9 2.6 fusion.15
  230.7 142.7 %all-reduce.7.cloned.1.call-done = f32[1,256,256]{2,1,0:T(8,128)} async-done(((f32[1,256,256]{2,1,0:T(8,128)}), f32[1,256,256]{2,1,0:T(8,128)}) %all-reduce.7.cloned.1.call-update) | async-done | bytes 262160 | tf_op jit(solution)/shard_map/psum | solution.py:47
  373.4 1.6 select_reduce_fusion.1
  375.6 1.6 multiply_reduce_fusion.1
  378.0 1.4 fusion.117
  386.3 2.3 fusion.7
  388.6 2.7 collective-permute-start.4
  391.4 18.7 %collective-permute-done.4 = f32[2048,128]{0,1:T(8,128)} collective-permute-done((f32[2048,128]{0,1:T(8,128)}, f32[2048,128]{0,1:T(8,128)}, u32[]{:S(2)}, u32[]{:S(2)}) %collective-permute-start.4) | collective-permute-done | bytes 1048608 | tf_op jit(solution)/shard_map/ppermute | solution.py:32
  410.1 1.7 broadcast_select_fusion.5
  411.8 2.6 fusion.16
  414.7 142.7 %all-reduce.9.cloned.1.call-done = f32[1,256,256]{2,1,0:T(8,128)} async-done(((f32[1,256,256]{2,1,0:T(8,128)}), f32[1,256,256]{2,1,0:T(8,128)}) %all-reduce.9.cloned.1.call-update) | async-done | bytes 262160 | tf_op jit(solution)/shard_map/psum | solution.py:47
  557.3 1.6 select_reduce_fusion
  559.6 1.6 multiply_reduce_fusion
  561.9 1.4 fusion.93
  571.6 1.8 fusion.268
  574.4 137.6 %all-reduce.11.cloned.1.call-done = f32[128,128]{1,0:T(8,128)} async-done(((f32[128,128]{1,0:T(8,128)}), f32[128,128]{1,0:T(8,128)}) %all-reduce.11.cloned.1.call-update) | async-done | bytes 65552 | tf_op jit(solution)/shard_map/psum | solution.py:88
  (78 shorter events, 29.6 us)
Async XLA Ops:
  7.2 564.4 %copy-start = (f32[32,64,128]{2,1,0:T(8,128)S(1)}, f32[32,64,128]{2,1,0:T(8,128)}, u32[]{:S(2)}) copy-start(f32[32,64,128]{2,1,0:T(8,128)} %param.9) | copy-start | bytes 3145732
  7.2 182.8 %all-reduce.5.cloned.1.call-start = ((), (), s32[]{:S(2)}) async-start(), calls=%async_computation | async-start | bytes 524288 | tf_op jit(solution)/shard_map/psum | solution.py:47
  9.5 14.7 %copy-start.4 = (f32[6]{0:T(128)S(1)}, f32[6]{0:T(128)}, u32[]{:S(2)}) copy-start(f32[6]{0:T(128)} %param.7) | copy-start | bytes 76
  18.6 6.4 collective-permute-start
  23.0 5.5 collective-permute-start.1
  35.9 2.0 copy-start.3
  35.9 4.4 collective-permute-start.2
  46.2 327.2 %all-reduce.7.cloned.1.call-start = ((), (), s32[]{:S(2)}) async-start(), calls=%async_computation.1 | async-start | bytes 524288 | tf_op jit(solution)/shard_map/psum | solution.py:47
  206.2 19.9 %collective-permute-start.3 = (f32[2048,128]{0,1:T(8,128)}, f32[2048,128]{0,1:T(8,128)}, u32[]{:S(2)}, u32[]{:S(2)}) collective-permute-start(f32[2048,128]{0,1:T(8,128)} %fusion.9), channel_id=1, source_target_pairs={{0,64},{64,0},{32,96},{96,32},{128,192},{192,128},{160,224},{224,1... | collective-permute-start | bytes 3145736 | tf_op jit(solution)/shard_map/ppermute | solution.py:32
  230.5 326.9 %all-reduce.9.cloned.1.call-start = ((), (), s32[]{:S(2)}) async-start(), calls=%async_computation.2 | async-start | bytes 524288 | tf_op jit(solution)/shard_map/psum | solution.py:47
  388.6 21.4 %collective-permute-start.4 = (f32[2048,128]{0,1:T(8,128)}, f32[2048,128]{0,1:T(8,128)}, u32[]{:S(2)}, u32[]{:S(2)}) collective-permute-start(f32[2048,128]{0,1:T(8,128)} %fusion.7), channel_id=1, source_target_pairs={{0,128},{128,0},{32,160},{160,32},{64,192},{192,64},{96,224},{224,... | collective-permute-start | bytes 3145736 | tf_op jit(solution)/shard_map/ppermute | solution.py:32
  411.8 151.6 %copy-start.1 = (f32[2048,128]{0,1:T(8,128)}, f32[2048,128]{0,1:T(8,128)S(1)}, u32[]{:S(2)}) copy-start(f32[2048,128]{0,1:T(8,128)S(1)} %get-tuple-element.5) | copy-start | bytes 3145732
  414.4 297.7 %all-reduce.11.cloned.1.call-start = ((), (), s32[]{:S(2)}) async-start(), calls=%async_computation.3 | async-start | bytes 131072 | tf_op jit(solution)/shard_map/psum | solution.py:88
  567.9 2.3 copy-start.2
Sparse Core Ops, SparseCore 0:
  46.3 143.6 all-reduce.4
  230.6 142.7 all-reduce.6
  414.5 142.7 all-reduce.8
  573.5 138.4 all-reduce.10
where the time goes:
time: 731 us; the launch traced here: 720 us
  waiting for transfers between devices  610 us (83%)
  matrix products  58.2 us (8%)
  between operations  18.8 us (3%)
  other arithmetic  15.7 us (2%)
  starting transfers between devices  12.4 us (2%)
    psum x3, waiting for transfers between devices, merge_level(): gram_total = lax.psum(partial_gram, 'space')  429 us
    psum x1, waiting for transfers between devices, local(): coefficients = lax.psum(partial_coef, 'space')  138 us
    ppermute x3, waiting for transfers between devices, partner(): return lax.ppermute(block, axis, route)  39.9 us
  transfers between devices with their start and end apart: 9, of which 8 were waited for; matrix products, arithmetic and copies ran while one was open for 0% of the time, Pallas kernels for 0%

commit v1 on v0

v1 whole, which is shorter than its diff:
```python
import functools

import jax
import jax.numpy as jnp
from jax import lax
from jax.experimental import pallas as pl
from jax.experimental.pallas import tpu as pltpu
from jax.sharding import PartitionSpec as P

SIGN_STEPS = 8
NX_CHIPS, NY_CHIPS, NZ_CHIPS = 4, 4, 8
COLS = 128
FIRST_ROWS, SECOND_ROWS = 3 * COLS, 10 * COLS
MESH = pl.DeviceIdType.MESH

exact_dot = lax.Precision.HIGHEST


def padded_2(x, sides, width):
    for axis, dim in sides:
        size, length = (lax.axis_size(axis), x.shape[dim])
        up = [(i, (i + 1) % size) for i in range(size - 1)]
        down = [(j, i) for i, j in up]
        last = lax.slice_in_dim(x, length - width, length, axis=dim)
        initial = lax.slice_in_dim(x, 0, width, axis=dim)
        before = lax.ppermute(last, axis, up)
        after = lax.ppermute(initial, axis, down)
        x = jnp.concatenate([before, x, after], axis=dim)
    return x


def band_matrix(tap_values, out_count, in_width, shift_by):
    row_ids = lax.broadcasted_iota(jnp.int32, (out_count, in_width), 0)
    col_ids = lax.broadcasted_iota(jnp.int32, (out_count, in_width), 1)
    tap_offset = col_ids - 2 * row_ids - shift_by
    band_table = jnp.zeros((out_count, in_width), jnp.float32)
    for tap_index in range(6):
        band_table = band_table + jnp.where(tap_offset == tap_index, tap_values[tap_index], 0.0)
    return band_table


def rows_at(start, size):
    return pl.ds(pl.multiple_of(start, 8), size)


NN = (((1,), (0,)), ((), ()))
TN = (((0,), (0,)), ((), ()))


def halves(a):
    high = a.astype(jnp.bfloat16)
    return high, (a - high.astype(jnp.float32)).astype(jnp.bfloat16)


def dot(a, b, dims):
    return lax.dot_general(a, b, dims, preferred_element_type=jnp.float32)


def dot3(a, b, dims=NN):
    (a_high, a_low), (b_high, b_low) = a, b
    return dot(a_high, b_high, dims) + (dot(a_high, b_low, dims) + dot(a_low, b_high, dims))


def mul(a, b, dims=NN):
    return dot3(halves(a), halves(b), dims)


def block_2x2(low, cross, high):
    return jnp.concatenate(
        [jnp.concatenate([low, cross], axis=1), jnp.concatenate([cross.T, high], axis=1)], axis=0
    )


def start_sign(gram, y_ref):
    order = gram.shape[0]
    identity = lax.broadcasted_iota(jnp.int32, gram.shape, 0) == lax.broadcasted_iota(jnp.int32, gram.shape, 1)
    mean_eig = jnp.sum(jnp.where(identity, gram, 0.0), keepdims=True) / order
    shifted = gram - jnp.where(identity, mean_eig, 0.0)
    y_ref[...] = shifted / jnp.sqrt(jnp.sum(shifted * shifted, keepdims=True) + 1e-06)


def sign_step(y_ref):
    y = y_ref[...]
    y_halves = halves(y)
    square = dot3(y_halves, y_halves)
    y_ref[...] = 1.5 * y - 0.5 * dot3(y_halves, halves(square))


def combine_of(y_ref):
    y = y_ref[...]
    order = y.shape[0]
    row = lax.broadcasted_iota(jnp.int32, (order, order // 2), 0)
    col = lax.broadcasted_iota(jnp.int32, (order, order // 2), 1)
    ones = jnp.where((row == col) | (row == col + order // 2), 0.5, 0.0)
    return ones + 0.5 * (y[:, : order // 2] + y[:, order // 2 :])


def run_signs(*refs):
    def body(step, carry):
        for ref in refs:
            sign_step(ref)
        return carry

    lax.fori_loop(0, SIGN_STEPS, body, 0)


def merge_kernel(factor, probes, pieces, coef, pair, cat_high, cat_low, gram, part1, gath1, cbuf1, zbuf1, xbuf1,
                 quarter, rows4, diag, part2, gath2, cbuf2, zbuf2, xbuf2, ybuf2, sign, probe_rows, turned, coef_all,
                 send, recv, local_sem):
    t = lax.axis_index("tm")
    s = lax.axis_index("space")
    y, core = t // 2, t % 2
    x, z = s // NZ_CHIPS, s % NZ_CHIPS
    half = factor.shape[0] // 2
    own_rows = half // NY_CHIPS

    def at(d_z=0, d_x=0, d_y=0, flip=0):
        c = (core + flip) % 2
        return {
            "tm": ((y + d_y) % NY_CHIPS) * 2 + c,
            "space": ((x + d_x) % NX_CHIPS) * NZ_CHIPS + (z + d_z) % NZ_CHIPS,
        }

    z_offsets = range(1, NZ_CHIPS)
    x_offsets = range(1, NX_CHIPS)
    y_offsets = range(1, NY_CHIPS)
    barrier = pltpu.get_barrier_semaphore()
    peers = [at(d_z=d) for d in z_offsets] + [at(d_x=d) for d in x_offsets]
    peers += [at(d_y=d, flip=f) for f in range(2) for d in range(NY_CHIPS) if d or f]
    for peer in peers:
        pl.semaphore_signal(barrier, inc=1, device_id=peer, device_id_type=MESH)

    count = [0]
    unsent = []

    def push(src, dst, to, landed):
        index = count[0]
        count[0] += 1

        def make(a, b):
            return pltpu.make_async_remote_copy(
                src_ref=a, dst_ref=b, send_sem=send.at[index], recv_sem=recv.at[index], device_id=to, device_id_type=MESH
            )

        out = make(src, dst)
        out.start()
        unsent.append(out)
        return make(landed, landed)

    def arrive(copies):
        for c in copies:
            c.wait_recv()

    take_probes = pltpu.make_async_copy(
        probes.at[rows_at(core * half + y * own_rows, own_rows)], probe_rows, local_sem.at[0]
    )
    take_probes.start()
    take_own = pltpu.make_async_copy(factor.at[rows_at(core * half, half)], pair.at[core], local_sem.at[1])
    take_own.start()
    pl.semaphore_wait(barrier, len(peers))
    arrive([push(factor.at[rows_at((1 - core) * half, half)], pair.at[core], at(flip=1), pair.at[1 - core])])
    take_own.wait()

    def all_sum(part, gath, cbuf, zbuf, xbuf, ybuf):
        rows = part.shape[0] // 2
        piece = rows // NZ_CHIPS
        mine = core * rows
        arrive([push(part.at[rows_at((1 - core) * rows, rows)], cbuf, at(flip=1), cbuf)])
        part[rows_at(mine, rows), :] = part[rows_at(mine, rows), :] + cbuf[...]
        arrive([
            push(part.at[rows_at(mine + (z + d) % NZ_CHIPS * piece, piece)], zbuf.at[d - 1], at(d_z=d), zbuf.at[d - 1])
            for d in z_offsets
        ])
        total = part[rows_at(mine + z * piece, piece), :]
        for d in z_offsets:
            total = total + zbuf[d - 1]
        xbuf[x] = total
        arrive([
            push(xbuf.at[x], xbuf.at[x], at(d_x=d), xbuf.at[(x + NX_CHIPS - d) % NX_CHIPS]) for d in x_offsets
        ])
        total = (xbuf[0] + xbuf[1]) + (xbuf[2] + xbuf[3])
        if ybuf is not None:
            ybuf[y] = total
            arrive([
                push(ybuf.at[y], ybuf.at[y], at(d_y=d), ybuf.at[(y + NY_CHIPS - d) % NY_CHIPS]) for d in y_offsets
            ])
            total = (ybuf[0] + ybuf[1]) + (ybuf[2] + ybuf[3])
        own = gath.at[rows_at(mine + z * piece, piece)]
        gath[rows_at(mine + z * piece, piece), :] = total
        arrive([
            push(own, own, at(d_z=d), gath.at[rows_at(mine + (z + NZ_CHIPS - d) % NZ_CHIPS * piece, piece)])
            for d in z_offsets
        ])
        ours, theirs = gath.at[rows_at(mine, rows)], gath.at[rows_at((1 - core) * rows, rows)]
        arrive([push(ours, ours, at(flip=1), theirs)])

    gram[...] = jnp.zeros_like(gram)

    def add_rows(chunk, carry):
        rows = rows_at(chunk * own_rows, own_rows)
        high, low = halves(jnp.concatenate([pair[0, rows, :], pair[1, rows, :]], axis=1))
        cat_high[rows, :] = high
        cat_low[rows, :] = low
        cross = dot(high, low, TN)
        gram[...] = gram[...] + (dot(high, high, TN) + (cross + cross.T))
        return carry

    lax.fori_loop(0, NY_CHIPS, add_rows, 0)
    part1[:COLS] = gram[:COLS, :COLS]
    part1[COLS : 2 * COLS] = gram[:COLS, COLS:]
    part1[2 * COLS :] = gram[COLS:, COLS:]
    all_sum(part1, gath1, cbuf1, zbuf1, xbuf1, None)
    total = block_2x2(gath1[:COLS], gath1[COLS : 2 * COLS], gath1[2 * COLS :])
    start_sign(total, sign.at[0])
    run_signs(sign.at[0])
    combine = combine_of(sign.at[0])
    combine_halves = halves(combine)

    came = []
    for d in [1, 2, 3, 0]:
        to = (y + d) % NY_CHIPS
        rows = rows_at(to * own_rows, own_rows)
        merged = dot3((cat_high[rows, :], cat_low[rows, :]), combine_halves)
        if d:
            quarter[d - 1] = merged
            came.append(push(quarter.at[d - 1], rows4.at[y], at(d_y=d), rows4.at[(y + NY_CHIPS - d) % NY_CHIPS]))
        else:
            rows4[y] = merged
    diag[y] = mul(combine, mul(total, combine), TN)
    diag_came = [
        push(diag.at[y], diag.at[y], at(d_y=d), diag.at[(y + NY_CHIPS - d) % NY_CHIPS]) for d in y_offsets
    ]
    take_probes.wait()
    arrive(came)

    f4 = [halves(rows4[p]) for p in range(NY_CHIPS)]
    probe_halves = halves(probe_rows[...])
    place = {(0, 1): 0, (2, 3): 1, (0, 2): 2, (0, 3): 3, (1, 2): 4, (1, 3): 5, (0, 4): 6, (1, 4): 7, (2, 4): 8, (3, 4): 9}
    right = f4 + [probe_halves]
    for p in range(NY_CHIPS):
        wide = tuple(jnp.concatenate([right[q][h] for q in range(p + 1, 5)], axis=1) for h in range(2))
        products = dot3(f4[p], wide, TN)
        for q in range(p + 1, 5):
            at_block = place[p, q] * COLS
            part2[at_block : at_block + COLS] = products[:, (q - p - 1) * COLS : (q - p) * COLS]
    all_sum(part2, gath2, cbuf2, zbuf2, xbuf2, ybuf2)
    arrive(diag_came)

    def summed(index):
        return gath2[index * COLS : (index + 1) * COLS]

    gram_low = block_2x2(diag[0], summed(0), diag[1])
    gram_high = block_2x2(diag[2], summed(1), diag[3])
    start_sign(gram_low, sign.at[0])
    start_sign(gram_high, sign.at[1])
    run_signs(sign.at[0], sign.at[1])
    low, high = combine_of(sign.at[0]), combine_of(sign.at[1])
    low_h, high_h = halves(low), halves(high)
    crossing = jnp.concatenate(
        [jnp.concatenate([summed(2), summed(3)], axis=1), jnp.concatenate([summed(4), summed(5)], axis=1)], axis=0
    )
    diag_low = dot3(low_h, halves(dot3(halves(gram_low), low_h)), TN)
    diag_high = dot3(high_h, halves(dot3(halves(gram_high), high_h)), TN)
    cross = dot3(low_h, halves(dot3(halves(crossing), high_h)), TN)

    start_sign(block_2x2(diag_low, cross, diag_high), sign.at[0])
    run_signs(sign.at[0])
    last = combine_of(sign.at[0])
    whole = halves(
        jnp.concatenate([dot3(low_h, halves(last[:COLS])), dot3(high_h, halves(last[COLS:]))], axis=0)
    )
    all4 = tuple(jnp.concatenate([f[h] for f in [halves(rows4[p]) for p in range(NY_CHIPS)]], axis=1) for h in range(2))
    basis = dot3(all4, whole)
    turned[...] = basis.T
    width = COLS // 8
    place_own = core * NY_CHIPS + y
    came = []
    for f in range(2):
        for d in range(NY_CHIPS):
            if d or f:
                to_t = ((y + d) % NY_CHIPS) * 2 + (core + f) % 2
                from_place = ((core + f) % 2) * NY_CHIPS + (y + NY_CHIPS - d) % NY_CHIPS
                came.append(
                    push(turned.at[rows_at(to_t * width, width)], pieces.at[place_own], at(d_y=d, flip=f), pieces.at[from_place])
                )
    pieces[place_own] = turned[rows_at(t * width, width), :]
    coef_all[...] = mul_pair(whole, gath2)
    coef[...] = coef_all[rows_at(t * width, width), :]
    arrive(came)
    for out in unsent:
        out.wait_send()


def mul_pair(whole, gath2):
    return dot3(whole, halves(gath2[6 * COLS :]), TN)


def merge_all(factor, probes):
    rows, cols = factor.shape
    half = rows // 2
    own_rows = half // NY_CHIPS
    f32, vmem = jnp.float32, pltpu.VMEM
    piece1, piece2 = FIRST_ROWS // 16, SECOND_ROWS // 16
    return pl.pallas_call(
        merge_kernel,
        out_shape=(
            jax.ShapeDtypeStruct((8, cols // 8, own_rows), f32),
            jax.ShapeDtypeStruct((cols // 8, cols), f32),
        ),
        in_specs=[pl.BlockSpec(memory_space=pltpu.VMEM), pl.BlockSpec(memory_space=pl.ANY)],
        out_specs=(pl.BlockSpec(memory_space=pltpu.VMEM), pl.BlockSpec(memory_space=pltpu.VMEM)),
        scratch_shapes=[
            vmem((2, half, cols), f32),
            vmem((half, 2 * cols), jnp.bfloat16),
            vmem((half, 2 * cols), jnp.bfloat16),
            vmem((2 * cols, 2 * cols), f32),
            vmem((FIRST_ROWS, cols), f32),
            vmem((FIRST_ROWS, cols), f32),
            vmem((FIRST_ROWS // 2, cols), f32),
            vmem((NZ_CHIPS - 1, piece1, cols), f32),
            vmem((NX_CHIPS, piece1, cols), f32),
            vmem((NY_CHIPS - 1, own_rows, cols), f32),
            vmem((NY_CHIPS, own_rows, cols), f32),
            vmem((NY_CHIPS, cols, cols), f32),
            vmem((SECOND_ROWS, cols), f32),
            vmem((SECOND_ROWS, cols), f32),
            vmem((SECOND_ROWS // 2, cols), f32),
            vmem((NZ_CHIPS - 1, piece2, cols), f32),
            vmem((NX_CHIPS, piece2, cols), f32),
            vmem((NY_CHIPS, piece2, cols), f32),
            vmem((2, 2 * cols, 2 * cols), f32),
            vmem((own_rows, cols), f32),
            vmem((cols, own_rows), f32),
            vmem((cols, cols), f32),
            pltpu.SemaphoreType.DMA((64,)),
            pltpu.SemaphoreType.DMA((64,)),
            pltpu.SemaphoreType.DMA((2,)),
        ],
        compiler_params=pltpu.CompilerParams(
            collective_id=1, has_side_effects=True, vmem_limit_bytes=32 << 20
        ),
        name="merge_all",
    )(factor, probes)


def local(snapshots, land_mask, taps_rows, taps_cols, probes):
    rows_dev, cell_cols, columns = snapshots.shape
    ocean_field = snapshots * land_mask.astype(jnp.float32)[:, :, None]
    across = band_matrix(taps_cols, cell_cols // 2, cell_cols, -2)
    narrowed = jnp.einsum("jy,xys->xjs", across, ocean_field, precision=exact_dot)
    padded = padded_2(narrowed, (("space", 0),), 3)
    row_filter = band_matrix(taps_rows, rows_dev // 2, rows_dev + 6, 1)
    filtered = jnp.einsum("ip,pjs->ijs", row_filter, padded, precision=exact_dot)
    cell_rows = rows_dev // 2 * (cell_cols // 2)
    factor = filtered.reshape(cell_rows, columns)
    flat_probes = probes.reshape(cell_rows, probes.shape[2])
    pieces, coef_own = merge_all(factor, flat_probes)
    basis_own = pieces.transpose(0, 2, 1)
    return (basis_own.reshape(rows_dev // 2, cell_cols // 2, columns // 8), coef_own)


def solution(mesh):
    placed = (P("space", None, "tm"), P("space", None), P(), P(), P("space", None, None))
    return jax.shard_map(
        local,
        mesh=mesh,
        in_specs=placed,
        out_specs=(P("space", None, "tm"), P("tm", None)),
        check_vma=False,
    )
```

time: 731 us -> 125 us (0.17); the launches traced: 720 us -> 125 us
  waiting for transfers between devices: 610 us -> 3.57 us
  Pallas kernels: 0 us -> 93.6 us
  matrix products: 58.2 us -> 15.6 us
  between operations: 18.8 us -> 0.74 us
  other arithmetic: 15.7 us -> 1.04 us
    psum x4 -> x0, waiting for transfers between devices: 567 us -> none  [the longest x3 429 us: merge_level(): gram_total = lax.psum(partial_gram, 'space')]
    pallas_call x0 -> x1, Pallas kernels: none -> 93.6 us  [merge_all(): pl.pallas_call(merge_kernel, out_shape=(jax.ShapeDtypeStruct((8, cols //...]
    dot_general x55 -> x0, matrix products: 42.7 us -> none  [the longest x24 12.3 us: merge_level(): jnp.einsum('gab,gbc->gac', sign_iter, square, precision=exact_dot)]
    ppermute x3 -> x0, waiting for transfers between devices: 39.9 us -> none  [partner(): return lax.ppermute(block, axis, route)]
    reduce_sum x6 -> x0, other arithmetic: 9.65 us -> none  [the longest x3 4.88 us: merge_level(): norm_scale = jnp.sqrt(jnp.sum(shifted * shifted, axis=(1, 2)) + 1e-06)]
  transfers between devices with their start and end apart: 9 -> 2, of which waited for: 8 -> 1; matrix products, arithmetic and copies ran while one was open for 0% -> 1% of each run, Pallas kernels for 0% -> 0%
where the time goes in v1:
time: 125 us
  Pallas kernels  93.6 us (75%)
  matrix products  15.6 us (12%)
  starting transfers between devices  5.66 us (5%)
  local copies, waits for them, and re-layouts  4.47 us (4%)
  waiting for transfers between devices  3.57 us (3%)
    pallas_call x1, Pallas kernels, merge_all(): pl.pallas_call(merge_kernel, out_shape=(jax.ShapeDtypeStruct((8, cols //...  93.6 us
    dot_general x1, matrix products, local(): jnp.einsum('jy,xys->xjs', across, ocean_field, precision=exact_dot)  9.02 us
    dot_general x1, matrix products, local(): jnp.einsum('ip,pjs->ijs', row_filter, padded, precision=exact_dot)  6.54 us
    ppermute x1, starting transfers between devices, padded_2(): before = lax.ppermute(last, axis, up)  4.36 us
    ppermute x1, waiting for transfers between devices, padded_2(): after = lax.ppermute(initial, axis, down)  3.56 us
  transfers between devices with their start and end apart: 2, of which 1 were waited for; matrix products, arithmetic and copies ran while one was open for 1% of the time, Pallas kernels for 0%

profile of v1, /device:TPU:1, one launch (start us, length us, event | category | flops | bytes accessed | tf_op | source)
XLA Modules:
  0.0 124.6 jit_solution(16018020962199837051)
XLA Ops:
  0.6 1.5 %fusion.102 = (f32[1]{0:T(128)}, f32[1]{0:T(128)}, f32[1]{0:T(128)}, f32[1]{0:T(128)}, f32[1]{0:T(128)}, /*index=5*/f32[1]{0:T(128)}) fusion(f32[6]{0:T(128)} %param.8), kind=kLoop, calls=%fused_computation.93 | loop fusion | bytes 48 | tf_op jit(solution)/shard_map/slice | solution.py:38
  2.2 0.8 convert_element_type.3
  2.9 0.0 copy-start.1
  2.9 9.0 %fusion.5 = f32[64,64,128]{2,1,0:T(8,128)S(1)} fusion(f32[64,128,128]{2,1,0:T(8,128)} %param.5, f32[64,128]{1,0:T(8,128)S(1)} %convert_element_type.3, f32[]{:T(128)} %bitcast.12, f32[]{:T(128)} %bitcast.11, f32[]{:T(128)} %bitcast.10, f32[]{:T(128)} %bitcast.9, f32[]{:T(128)} %bitcast.8, f32[]{:T(128)} %bitcast.7, s32[64]{0:T(128)S(1)} %iota_multiply_fusion), kind=kOutput, calls=%fused_computation.6 | convolution fusion | flops 806510592 | bytes 6324504 | tf_op jit(solution)/shard_map/jy,xys->xjs/dot_general | solution.py:350
  12.0 4.4 %collective-permute-start = (f32[3,64,128]{2,1,0:T(8,128)S(1)}, f32[3,64,128]{2,1,0:T(8,128)S(1)}, u32[]{:S(2)}, u32[]{:S(2)}) collective-permute-start(f32[3,64,128]{2,1,0:T(8,128)S(1)} %get-tuple-element.8), channel_id=1, source_target_pairs={{0,1},{1,2},{2,3},{3,4},{4,5},{5,6},{6,7},{7,8},{8,9},{9,10},{10,1... | collective-permute-start | bytes 294920 | tf_op jit(solution)/shard_map/ppermute | solution.py:26
  16.4 1.3 %collective-permute-start.1 = (f32[3,64,128]{2,1,0:T(8,128)S(1)}, f32[3,64,128]{2,1,0:T(8,128)S(1)}, u32[]{:S(2)}, u32[]{:S(2)}) collective-permute-start(f32[3,64,128]{2,1,0:T(8,128)S(1)} %get-tuple-element.9), channel_id=1, source_target_pairs={{1,0},{2,1},{3,2},{4,3},{5,4},{6,5},{7,6},{8,7},{9,8},{10,9},{11,1... | collective-permute-start | bytes 294920 | tf_op jit(solution)/shard_map/ppermute | solution.py:27
  17.7 0.0 copy-done.1
  17.7 0.7 fusion.101
  18.3 0.0 collective-permute-done
  18.3 3.6 %collective-permute-done.1 = f32[3,64,128]{2,1,0:T(8,128)S(1)} collective-permute-done((f32[3,64,128]{2,1,0:T(8,128)S(1)}, f32[3,64,128]{2,1,0:T(8,128)S(1)}, u32[]{:S(2)}, u32[]{:S(2)}) %collective-permute-start.1) | collective-permute-done | bytes 98336 | tf_op jit(solution)/shard_map/ppermute | solution.py:27
  21.9 0.3 pad_maximum_fusion
  22.2 0.0 copy-start
  22.2 6.5 %fusion.2 = f32[32,64,128]{2,0,1:T(8,128)S(1)} fusion(f32[70,64,128]{2,1,0:T(8,128)S(1)} %pad_maximum_fusion, f32[]{:T(128)} %bitcast.5, f32[]{:T(128)} %bitcast.4, f32[]{:T(128)} %bitcast.3, f32[]{:T(128)} %bitcast.2, f32[]{:T(128)} %bitcast.1, f32[]{:T(128)} %bitcast, s32[32]{0:T(128)S(1)} %iota_multiply_fusion.1), kind=kOutput, calls=%fused_computation.2 | convolution fusion | flops 220243520 | bytes 3342488 | tf_op jit(solution)/shard_map/ip,pjs->ijs/dot_general | solution.py:353
  28.7 0.6 copy.10
  29.4 0.0 copy-done
  29.4 93.6 %merge_all.1 = (f32[8,16,256]{2,1,0:T(8,128)S(1)}, f32[16,128]{1,0:T(8,128)S(1)}) custom-call(f32[2048,128]{1,0:T(8,128)S(1)} %bitcast.25, f32[2048,128]{1,0:T(8,128)S(1)} %bitcast.26), custom_call_target="tpu_custom_call" | custom-call | tf_op jit(solution)/shard_map/merge_all/pallas_call | solution.py:304
  123.0 0.1 copy.11
  123.0 0.1 reshape.16
  123.1 0.9 copy.12
  124.0 0.6 copy.16
  (3 shorter events, 0.0 us)
Async XLA Ops:
  2.9 14.7 %copy-start.1 = (f32[6]{0:T(128)S(1)}, f32[6]{0:T(128)}, u32[]{:S(2)}) copy-start(f32[6]{0:T(128)} %param.7) | copy-start | bytes 76
  12.0 6.4 %collective-permute-start = (f32[3,64,128]{2,1,0:T(8,128)S(1)}, f32[3,64,128]{2,1,0:T(8,128)S(1)}, u32[]{:S(2)}, u32[]{:S(2)}) collective-permute-start(f32[3,64,128]{2,1,0:T(8,128)S(1)} %get-tuple-element.8), channel_id=1, source_target_pairs={{0,1},{1,2},{2,3},{3,4},{4,5},{5,6},{6,7},{7,8},{8,9},{9,10},{10,1... | collective-permute-start | bytes 294920 | tf_op jit(solution)/shard_map/ppermute | solution.py:26
  16.4 5.5 %collective-permute-start.1 = (f32[3,64,128]{2,1,0:T(8,128)S(1)}, f32[3,64,128]{2,1,0:T(8,128)S(1)}, u32[]{:S(2)}, u32[]{:S(2)}) collective-permute-start(f32[3,64,128]{2,1,0:T(8,128)S(1)} %get-tuple-element.9), channel_id=1, source_target_pairs={{1,0},{2,1},{3,2},{4,3},{5,4},{6,5},{7,6},{8,7},{9,8},{10,9},{11,1... | collective-permute-start | bytes 294920 | tf_op jit(solution)/shard_map/ppermute | solution.py:27
  22.2 7.2 %copy-start = (f32[32,64,128]{2,1,0:T(8,128)S(1)}, f32[32,64,128]{2,1,0:T(8,128)}, u32[]{:S(2)}) copy-start(f32[32,64,128]{2,1,0:T(8,128)} %param.9) | copy-start | bytes 3145732

commit v2 on v1

--- a/solution.py
+++ b/solution.py
@@ -9,35 +9,11 @@
 
 SIGN_STEPS = 8
 NX_CHIPS, NY_CHIPS, NZ_CHIPS = 4, 4, 8
+SPACE = NX_CHIPS * NZ_CHIPS
 COLS = 128
 FIRST_ROWS, SECOND_ROWS = 3 * COLS, 10 * COLS
+TAPS, CHUNK, EDGE = 6, 8, 8
 MESH = pl.DeviceIdType.MESH
-
-exact_dot = lax.Precision.HIGHEST
-
-
-def padded_2(x, sides, width):
-    for axis, dim in sides:
-        size, length = (lax.axis_size(axis), x.shape[dim])
-        up = [(i, (i + 1) % size) for i in range(size - 1)]
-        down = [(j, i) for i, j in up]
-        last = lax.slice_in_dim(x, length - width, length, axis=dim)
-        initial = lax.slice_in_dim(x, 0, width, axis=dim)
-        before = lax.ppermute(last, axis, up)
-        after = lax.ppermute(initial, axis, down)
-        x = jnp.concatenate([before, x, after], axis=dim)
-    return x
-
-
-def band_matrix(tap_values, out_count, in_width, shift_by):
-    row_ids = lax.broadcasted_iota(jnp.int32, (out_count, in_width), 0)
-    col_ids = lax.broadcasted_iota(jnp.int32, (out_count, in_width), 1)
-    tap_offset = col_ids - 2 * row_ids - shift_by
-    band_table = jnp.zeros((out_count, in_width), jnp.float32)
-    for tap_index in range(6):
-        band_table = band_table + jnp.where(tap_offset == tap_index, tap_values[tap_index], 0.0)
-    return band_table
-
 
 def rows_at(start, size):
     return pl.ds(pl.multiple_of(start, 8), size)
@@ -104,14 +80,18 @@
     lax.fori_loop(0, SIGN_STEPS, body, 0)
 
 
-def merge_kernel(factor, probes, pieces, coef, pair, cat_high, cat_low, gram, part1, gath1, cbuf1, zbuf1, xbuf1,
+def merge_kernel(snapshots, mask, taps_rows, taps_cols, probes, pieces, coef,
+                 field, mask_own, mask_ends, tall, away, pair, cat_high, cat_low, gram, part1, gath1, cbuf1, zbuf1, xbuf1,
                  quarter, rows4, diag, part2, gath2, cbuf2, zbuf2, xbuf2, ybuf2, sign, probe_rows, turned, coef_all,
-                 send, recv, local_sem):
+                 send, recv, local_sem, chunk_sem):
     t = lax.axis_index("tm")
     s = lax.axis_index("space")
     y, core = t // 2, t % 2
     x, z = s // NZ_CHIPS, s % NZ_CHIPS
-    half = factor.shape[0] // 2
+    rows_dev, cells = snapshots.shape[0], snapshots.shape[1]
+    out_rows, out_cells = rows_dev // 2, cells // 2
+    half = out_rows * out_cells // 2
+    chunks = rows_dev // CHUNK
     own_rows = half // NY_CHIPS
 
     def at(d_z=0, d_x=0, d_y=0, flip=0):
@@ -124,9 +104,12 @@
     z_offsets = range(1, NZ_CHIPS)
     x_offsets = range(1, NX_CHIPS)
     y_offsets = range(1, NY_CHIPS)
+    s_above, s_below = (s + SPACE - 1) % SPACE, (s + 1) % SPACE
+    above, below = {"tm": t, "space": s_above}, {"tm": t, "space": s_below}
     barrier = pltpu.get_barrier_semaphore()
     peers = [at(d_z=d) for d in z_offsets] + [at(d_x=d) for d in x_offsets]
     peers += [at(d_y=d, flip=f) for f in range(2) for d in range(NY_CHIPS) if d or f]
+    peers += [above, below]
     for peer in peers:
         pl.semaphore_signal(barrier, inc=1, device_id=peer, device_id_type=MESH)
 
@@ -155,11 +138,96 @@
         probes.at[rows_at(core * half + y * own_rows, own_rows)], probe_rows, local_sem.at[0]
     )
     take_probes.start()
-    take_own = pltpu.make_async_copy(factor.at[rows_at(core * half, half)], pair.at[core], local_sem.at[1])
-    take_own.start()
+    take_mask = pltpu.make_async_copy(mask, mask_own.at[pl.ds(0, rows_dev)], local_sem.at[1])
+    take_mask.start()
+
+    def chunk_copy(k):
+        first = (core * k + (1 - core) * (chunks - 1 - k)) * CHUNK
+        return pltpu.make_async_copy(
+            snapshots.at[pl.ds(first, CHUNK)], field.at[pl.ds(first + 2, CHUNK)], chunk_sem.at[k]
+        )
+
+    for k in range(chunks):
+        chunk_copy(k).start()
+    mask_own[rows_dev:, :] = jnp.zeros((COLS - rows_dev, cells), jnp.int32)
+    tall[:, :EDGE] = jnp.zeros((tall.shape[0], EDGE, COLS), jnp.float32)
+    tall[:, EDGE + cells :] = jnp.zeros((tall.shape[0], EDGE, COLS), jnp.float32)
+    take_mask.wait()
+    mask_cols = mask_own[...].astype(jnp.float32).T
+
+    def mask_chunk(k):
+        chunk_copy(k).wait()
+        first = (core * k + (1 - core) * (chunks - 1 - k)) * CHUNK
+        turned_mask = pltpu.roll(mask_cols, (COLS - first) % COLS, axis=1)
+        for r in range(CHUNK):
+            field[first + 2 + r] = field[first + 2 + r] * turned_mask[:, r : r + 1]
+
+    tr = [taps_rows[k] for k in range(TAPS)]
+    tc = [taps_cols[k] for k in range(TAPS)]
+
+    def filter_row(i, slot):
+        total = tr[0] * field[2 * i]
+        for k in range(1, TAPS):
+            total = total + tr[k] * field[2 * i + k]
+        tall[slot, EDGE : EDGE + cells] = total
+        out = tc[0] * tall[slot, pl.ds(EDGE - 2, out_cells, stride=2), :]
+        for k in range(1, TAPS):
+            out = out + tc[k] * tall[slot, pl.ds(EDGE - 2 + k, out_cells, stride=2), :]
+        return out
+
+    def filter_rows(first, store):
+        def body(step, carry):
+            for slot in range(tall.shape[0]):
+                n = step * tall.shape[0] + slot
+                store(n, filter_row(first + n, slot))
+            return carry
+
+        lax.fori_loop(0, (out_rows // 2 - 1) // tall.shape[0], body, 0)
+
+    def store_away(n, value):
+        away[rows_at((n + core) * out_cells, out_cells), :] = value
+
+    def store_own(n, value):
+        pair[core, rows_at((n + 1 - core) * out_cells, out_cells), :] = value
+
+    inner = half - out_cells
+    for k in range(chunks // 2 + 1):
+        mask_chunk(k)
     pl.semaphore_wait(barrier, len(peers))
-    arrive([push(factor.at[rows_at((1 - core) * half, half)], pair.at[core], at(flip=1), pair.at[1 - core])])
-    take_own.wait()
+    came = [
+        push(snapshots.at[pl.ds(rows_dev - 2, 2)], field.at[pl.ds(0, 2)], below, field.at[pl.ds(0, 2)]),
+        push(snapshots.at[pl.ds(0, 2)], field.at[pl.ds(rows_dev + 2, 2)], above, field.at[pl.ds(rows_dev + 2, 2)]),
+        push(mask.at[pl.ds(rows_dev - 8, 8)], mask_ends.at[pl.ds(0, 8)], below, mask_ends.at[pl.ds(0, 8)]),
+        push(mask.at[pl.ds(0, 8)], mask_ends.at[pl.ds(8, 8)], above, mask_ends.at[pl.ds(8, 8)]),
+    ]
+    filter_rows(1 + (out_rows // 2 - 1) * (1 - core), store_away)
+    crossed = [
+        push(
+            away.at[rows_at(core * out_cells, inner)],
+            pair.at[core, rows_at(core * out_cells, inner)],
+            at(flip=1),
+            pair.at[1 - core, rows_at((1 - core) * out_cells, inner)],
+        )
+    ]
+    for k in range(chunks // 2 + 1, chunks):
+        mask_chunk(k)
+    filter_rows(1 + (out_rows // 2 - 1) * core, store_own)
+    arrive(came)
+    ends = mask_ends[...].astype(jnp.float32)
+    ends = jnp.concatenate(
+        [jnp.where(s > 0, ends[:8], 0.0), jnp.where(s < SPACE - 1, ends[8:], 0.0), jnp.zeros((COLS - 16, cells), jnp.float32)],
+        axis=0,
+    ).T
+    for row, lane in ((0, 6), (1, 7), (rows_dev + 2, 8), (rows_dev + 3, 9)):
+        field[row] = field[row] * ends[:, lane : lane + 1]
+    last_away = rows_at((out_rows // 2 - 1) * out_cells * (1 - core), out_cells)
+    last_own = rows_at((out_rows // 2 - 1) * out_cells * core, out_cells)
+    away[last_away, :] = filter_row((out_rows - 1) * (1 - core), 0)
+    crossed.append(
+        push(away.at[last_away], pair.at[core, last_away], at(flip=1), pair.at[1 - core, last_own])
+    )
+    pair[core, last_own, :] = filter_row((out_rows - 1) * core, 1)
+    arrive(crossed)
 
     def all_sum(part, gath, cbuf, zbuf, xbuf, ybuf):
         rows = part.shape[0] // 2
@@ -295,8 +363,9 @@
     return dot3(whole, halves(gath2[6 * COLS :]), TN)
 
 
-def merge_all(factor, probes):
-    rows, cols = factor.shape
+def merge_all(snapshots, mask, taps_rows, taps_cols, probes):
+    rows_dev, cells, cols = snapshots.shape
+    rows = rows_dev // 2 * (cells // 2)
     half = rows // 2
     own_rows = half // NY_CHIPS
     f32, vmem = jnp.float32, pltpu.VMEM
@@ -307,9 +376,16 @@
             jax.ShapeDtypeStruct((8, cols // 8, own_rows), f32),
             jax.ShapeDtypeStruct((cols // 8, cols), f32),
         ),
-        in_specs=[pl.BlockSpec(memory_space=pltpu.VMEM), pl.BlockSpec(memory_space=pl.ANY)],
+        in_specs=[pl.BlockSpec(memory_space=pl.ANY)] * 2
+        + [pl.BlockSpec(memory_space=pltpu.SMEM)] * 2
+        + [pl.BlockSpec(memory_space=pl.ANY)],
         out_specs=(pl.BlockSpec(memory_space=pltpu.VMEM), pl.BlockSpec(memory_space=pltpu.VMEM)),
         scratch_shapes=[
+            vmem((rows_dev + 4, cells, cols), f32),
+            vmem((COLS, cells), jnp.int32),
+            vmem((16, cells), jnp.int32),
+            vmem((3, cells + 2 * EDGE, cols), f32),
+            vmem((half, cols), f32),
             vmem((2, half, cols), f32),
             vmem((half, 2 * cols), jnp.bfloat16),
             vmem((half, 2 * cols), jnp.bfloat16),
@@ -335,26 +411,20 @@
             pltpu.SemaphoreType.DMA((64,)),
             pltpu.SemaphoreType.DMA((64,)),
             pltpu.SemaphoreType.DMA((2,)),
+            pltpu.SemaphoreType.DMA((rows_dev // CHUNK,)),
         ],
         compiler_params=pltpu.CompilerParams(
             collective_id=1, has_side_effects=True, vmem_limit_bytes=32 << 20
         ),
         name="merge_all",
-    )(factor, probes)
+    )(snapshots, mask, taps_rows, taps_cols, probes)
 
 
 def local(snapshots, land_mask, taps_rows, taps_cols, probes):
     rows_dev, cell_cols, columns = snapshots.shape
-    ocean_field = snapshots * land_mask.astype(jnp.float32)[:, :, None]
-    across = band_matrix(taps_cols, cell_cols // 2, cell_cols, -2)
-    narrowed = jnp.einsum("jy,xys->xjs", across, ocean_field, precision=exact_dot)
-    padded = padded_2(narrowed, (("space", 0),), 3)
-    row_filter = band_matrix(taps_rows, rows_dev // 2, rows_dev + 6, 1)
-    filtered = jnp.einsum("ip,pjs->ijs", row_filter, padded, precision=exact_dot)
     cell_rows = rows_dev // 2 * (cell_cols // 2)
-    factor = filtered.reshape(cell_rows, columns)
     flat_probes = probes.reshape(cell_rows, probes.shape[2])
-    pieces, coef_own = merge_all(factor, flat_probes)
+    pieces, coef_own = merge_all(snapshots, land_mask, taps_rows, taps_cols, flat_probes)
     basis_own = pieces.transpose(0, 2, 1)
     return (basis_own.reshape(rows_dev // 2, cell_cols // 2, columns // 8), coef_own)
 

time: 125 us -> 106 us (0.85)
  matrix products: 15.6 us -> 0 us
  starting transfers between devices: 5.66 us -> 0 us
  Pallas kernels: 93.6 us -> 97.9 us
  waiting for transfers between devices: 3.57 us -> 0 us
  local copies, waits for them, and re-layouts: 4.47 us -> 7.11 us
    dot_general x2 -> x0, matrix products: 15.6 us -> none  [the longest x1 9.02 us: local(): jnp.einsum('jy,xys->xjs', across, ocean_field, precision=exact_dot)]
    ppermute x2 -> x0, starting transfers between devices: 5.66 us -> none  [the longest x1 4.36 us: padded_2(): before = lax.ppermute(last, axis, up)]
    unnamed x6 -> x12, local copies, waits for them, and re-layouts: 1.47 us -> 6.93 us
    pallas_call x1, Pallas kernels: 93.6 us -> 97.9 us  [merge_all(): pl.pallas_call(merge_kernel, out_shape=(jax.ShapeDtypeStruct((8, cols //...]
    ppermute x2 -> x0, waiting for transfers between devices: 3.57 us -> none  [the longest x1 3.56 us: padded_2(): after = lax.ppermute(initial, axis, down)]
    slice x3 -> x0, local copies, waits for them, and re-layouts: 2.22 us -> none  [the longest x2 2.2 us: band_matrix(): tap_values[tap_index]]
  transfers between devices with their start and end apart: 2 -> 0, of which waited for: 1 -> 0; matrix products, arithmetic and copies ran while one was open for 1% -> 0% of each run, Pallas kernels for 0% -> 0%
where the time goes in v2:
time: 106 us
  Pallas kernels  97.9 us (92%)
  local copies, waits for them, and re-layouts  7.11 us (7%)
    pallas_call x1, Pallas kernels, merge_all(): pl.pallas_call(merge_kernel, out_shape=(jax.ShapeDtypeStruct((8, cols //...  97.9 us
    unnamed x12, local copies, waits for them, and re-layouts  6.93 us

profile of v2, /device:TPU:1, one launch (start us, length us, event | category | flops | bytes accessed | tf_op | source)
XLA Modules:
  0.0 105.7 jit_solution(14546257028768818607)
XLA Ops:
  0.6 0.0 copy-start
  0.6 2.2 %copy-done = f32[64,128,128]{2,1,0:T(8,128)S(1)} copy-done((f32[64,128,128]{2,1,0:T(8,128)S(1)}, f32[64,128,128]{2,1,0:T(8,128)}, u32[]{:S(2)}) %copy-start) | copy-done | bytes 4194328
  2.8 0.0 copy-start.1
  2.8 1.2 %copy-done.1 = f32[32,64,128]{2,1,0:T(8,128)S(1)} copy-done((f32[32,64,128]{2,1,0:T(8,128)S(1)}, f32[32,64,128]{2,1,0:T(8,128)}, u32[]{:S(2)}) %copy-start.1) | copy-done | bytes 1048600
  4.0 0.0 copy-start.2
  4.0 0.8 copy-done.2
  4.8 0.0 copy-start.3
  4.8 0.7 copy-done.3
  5.5 0.0 copy-start.4
  5.5 0.7 copy-done.4
  6.1 97.9 %merge_all.1 = (f32[8,16,256]{2,1,0:T(8,128)S(1)}, f32[16,128]{1,0:T(8,128)S(1)}) custom-call(f32[64,128,128]{2,1,0:T(8,128)S(1)} %copy-done, s32[64,128]{1,0:T(8,128)S(1)} %copy-done.2, f32[6]{0:T(128)S(1)} %copy-done.3, f32[6]{0:T(128)S(1)} %copy-done.4, f32[2048,128]{1,0:T(8,128)S(1)} %bitcast.4), custom_call_target="tpu_custom_call" | custom-call | tf_op jit(solution)/shard_map/merge_all/pallas_call | solution.py:373
  104.0 0.1 copy.7
  104.1 0.1 reshape.11
  104.2 0.9 copy.8
  105.1 0.6 copy.10
Async XLA Ops:
  0.6 2.2 %copy-start = (f32[64,128,128]{2,1,0:T(8,128)S(1)}, f32[64,128,128]{2,1,0:T(8,128)}, u32[]{:S(2)}) copy-start(f32[64,128,128]{2,1,0:T(8,128)} %snapshots.1) | copy-start | bytes 12582916
  2.8 1.2 %copy-start.1 = (f32[32,64,128]{2,1,0:T(8,128)S(1)}, f32[32,64,128]{2,1,0:T(8,128)}, u32[]{:S(2)}) copy-start(f32[32,64,128]{2,1,0:T(8,128)} %param.9) | copy-start | bytes 3145732
  4.0 0.8 copy-start.2
  4.8 0.7 copy-start.3
  5.5 0.7 copy-start.4

commit v3 on v2

--- a/solution.py
+++ b/solution.py
@@ -9,9 +9,9 @@
 
 SIGN_STEPS = 8
 NX_CHIPS, NY_CHIPS, NZ_CHIPS = 4, 4, 8
-SPACE = NX_CHIPS * NZ_CHIPS
+SPACE, XY_CHIPS = NX_CHIPS * NZ_CHIPS, NX_CHIPS * NY_CHIPS
 COLS = 128
-FIRST_ROWS, SECOND_ROWS = 3 * COLS, 10 * COLS
+FIRST_ROWS, SECOND_ROWS, LATER_ROWS = 3 * COLS, 2 * COLS, 8 * COLS
 TAPS, CHUNK, EDGE = 6, 8, 8
 MESH = pl.DeviceIdType.MESH
 
@@ -71,18 +71,19 @@
     return ones + 0.5 * (y[:, : order // 2] + y[:, order // 2 :])
 
 
-def run_signs(*refs):
+def run_signs(steps, *refs):
     def body(step, carry):
         for ref in refs:
             sign_step(ref)
         return carry
 
-    lax.fori_loop(0, SIGN_STEPS, body, 0)
+    lax.fori_loop(0, steps, body, 0)
 
 
 def merge_kernel(snapshots, mask, taps_rows, taps_cols, probes, pieces, coef,
-                 field, mask_own, mask_ends, tall, away, pair, cat_high, cat_low, gram, part1, gath1, cbuf1, zbuf1, xbuf1,
-                 quarter, rows4, diag, part2, gath2, cbuf2, zbuf2, xbuf2, ybuf2, sign, probe_rows, turned, coef_all,
+                 row_taps, col_taps, field, mask_own, mask_ends, tall, away, pair, cat_high, cat_low, gram, part1, gath1, cbuf1, zbuf1, xbuf1,
+                 quarter, rows4, diag, part2, gath2, cbuf2, rbuf2, zbuf2,
+                 part3, gath3, cbuf3, rbuf3, zbuf3, sign, probe_rows, turned, coef_all,
                  send, recv, local_sem, chunk_sem):
     t = lax.axis_index("tm")
     s = lax.axis_index("space")
@@ -107,8 +108,9 @@
     s_above, s_below = (s + SPACE - 1) % SPACE, (s + 1) % SPACE
     above, below = {"tm": t, "space": s_above}, {"tm": t, "space": s_below}
     barrier = pltpu.get_barrier_semaphore()
-    peers = [at(d_z=d) for d in z_offsets] + [at(d_x=d) for d in x_offsets]
-    peers += [at(d_y=d, flip=f) for f in range(2) for d in range(NY_CHIPS) if d or f]
+    xy_offsets = [(a, b) for a in range(NX_CHIPS) for b in range(NY_CHIPS) if a or b]
+    peers = [at(d_z=d) for d in z_offsets] + [at(d_x=a, d_y=b) for a, b in xy_offsets]
+    peers += [at(d_y=d, flip=1) for d in range(NY_CHIPS)]
     peers += [above, below]
     for peer in peers:
         pl.semaphore_signal(barrier, inc=1, device_id=peer, device_id_type=MESH)
@@ -140,6 +142,12 @@
     take_probes.start()
     take_mask = pltpu.make_async_copy(mask, mask_own.at[pl.ds(0, rows_dev)], local_sem.at[1])
     take_mask.start()
+    take_taps = [
+        pltpu.make_async_copy(taps_rows, row_taps, local_sem.at[2]),
+        pltpu.make_async_copy(taps_cols, col_taps, local_sem.at[3]),
+    ]
+    for taps in take_taps:
+        taps.start()
 
     def chunk_copy(k):
         first = (core * k + (1 - core) * (chunks - 1 - k)) * CHUNK
@@ -162,8 +170,10 @@
         for r in range(CHUNK):
             field[first + 2 + r] = field[first + 2 + r] * turned_mask[:, r : r + 1]
 
-    tr = [taps_rows[k] for k in range(TAPS)]
-    tc = [taps_cols[k] for k in range(TAPS)]
+    for taps in take_taps:
+        taps.wait()
+    tr = [row_taps[k] for k in range(TAPS)]
+    tc = [col_taps[k] for k in range(TAPS)]
 
     def filter_row(i, slot):
         total = tr[0] * field[2 * i]
@@ -229,7 +239,7 @@
     pair[core, last_own, :] = filter_row((out_rows - 1) * core, 1)
     arrive(crossed)
 
-    def all_sum(part, gath, cbuf, zbuf, xbuf, ybuf):
+    def plane_sum(part, gath, cbuf, zbuf, xbuf):
         rows = part.shape[0] // 2
         piece = rows // NZ_CHIPS
         mine = core * rows
@@ -247,12 +257,6 @@
             push(xbuf.at[x], xbuf.at[x], at(d_x=d), xbuf.at[(x + NX_CHIPS - d) % NX_CHIPS]) for d in x_offsets
         ])
         total = (xbuf[0] + xbuf[1]) + (xbuf[2] + xbuf[3])
-        if ybuf is not None:
-            ybuf[y] = total
-            arrive([
-                push(ybuf.at[y], ybuf.at[y], at(d_y=d), ybuf.at[(y + NY_CHIPS - d) % NY_CHIPS]) for d in y_offsets
-            ])
-            total = (ybuf[0] + ybuf[1]) + (ybuf[2] + ybuf[3])
         own = gath.at[rows_at(mine + z * piece, piece)]
         gath[rows_at(mine + z * piece, piece), :] = total
         arrive([
@@ -262,6 +266,61 @@
         ours, theirs = gath.at[rows_at(mine, rows)], gath.at[rows_at((1 - core) * rows, rows)]
         arrive([push(ours, ours, at(flip=1), theirs)])
 
+    class WholeSum:
+        def __init__(self, part, gath, cbuf, rbuf, zbuf):
+            self.part, self.gath, self.cbuf, self.rbuf, self.zbuf = part, gath, cbuf, rbuf, zbuf
+            self.rows = part.shape[0] // 2
+            self.piece = self.rows // XY_CHIPS
+            self.ours = rows_at(core * self.rows, self.rows)
+            self.theirs = rows_at((1 - core) * self.rows, self.rows)
+
+        def piece_of(self, a, b):
+            owner = (x + a) % NX_CHIPS * NY_CHIPS + (y + b) % NY_CHIPS
+            return rows_at(core * self.rows + owner * self.piece, self.piece)
+
+        def start(self):
+            self.came = [push(self.part.at[self.theirs], self.cbuf, at(flip=1), self.cbuf)]
+
+        def scatter(self):
+            arrive(self.came)
+            self.part[self.ours, :] = self.part[self.ours, :] + self.cbuf[...]
+            self.came = [
+                push(self.part.at[self.piece_of(a, b)], self.rbuf.at[n], at(d_x=a, d_y=b), self.rbuf.at[n])
+                for n, (a, b) in enumerate(xy_offsets)
+            ]
+
+        def along_z(self):
+            arrive(self.came)
+            total = self.part[self.piece_of(0, 0), :]
+            for n in range(len(xy_offsets)):
+                total = total + self.rbuf[n]
+            self.zbuf[z] = total
+            self.came = [
+                push(self.zbuf.at[z], self.zbuf.at[z], at(d_z=d), self.zbuf.at[(z + NZ_CHIPS - d) % NZ_CHIPS])
+                for d in z_offsets
+            ]
+
+        def gather(self):
+            arrive(self.came)
+            terms = [self.zbuf[k] for k in range(NZ_CHIPS)]
+            while len(terms) > 1:
+                terms = [terms[k] + terms[k + 1] for k in range(0, len(terms), 2)]
+            own = self.piece_of(0, 0)
+            self.gath[own, :] = terms[0]
+            own = self.gath.at[own]
+            self.came = [
+                push(own, own, at(d_x=a, d_y=b), self.gath.at[self.piece_of(NX_CHIPS - a, NY_CHIPS - b)])
+                for a, b in xy_offsets
+            ]
+
+        def share(self):
+            arrive(self.came)
+            ours, theirs = self.gath.at[self.ours], self.gath.at[self.theirs]
+            self.came = [push(ours, ours, at(flip=1), theirs)]
+
+        def finish(self):
+            arrive(self.came)
+
     gram[...] = jnp.zeros_like(gram)
 
     def add_rows(chunk, carry):
@@ -277,10 +336,10 @@
     part1[:COLS] = gram[:COLS, :COLS]
     part1[COLS : 2 * COLS] = gram[:COLS, COLS:]
     part1[2 * COLS :] = gram[COLS:, COLS:]
-    all_sum(part1, gath1, cbuf1, zbuf1, xbuf1, None)
+    plane_sum(part1, gath1, cbuf1, zbuf1, xbuf1)
     total = block_2x2(gath1[:COLS], gath1[COLS : 2 * COLS], gath1[2 * COLS :])
     start_sign(total, sign.at[0])
-    run_signs(sign.at[0])
+    run_signs(SIGN_STEPS, sign.at[0])
     combine = combine_of(sign.at[0])
     combine_halves = halves(combine)
 
@@ -303,44 +362,71 @@
 
     f4 = [halves(rows4[p]) for p in range(NY_CHIPS)]
     probe_halves = halves(probe_rows[...])
-    place = {(0, 1): 0, (2, 3): 1, (0, 2): 2, (0, 3): 3, (1, 2): 4, (1, 3): 5, (0, 4): 6, (1, 4): 7, (2, 4): 8, (3, 4): 9}
+    sum_now = WholeSum(part2, gath2, cbuf2, rbuf2, zbuf2)
+    sum_later = WholeSum(part3, gath3, cbuf3, rbuf3, zbuf3)
+    part2[:COLS] = dot3(f4[0], f4[1], TN)
+    part2[COLS:] = dot3(f4[2], f4[3], TN)
+    sum_now.start()
+    place = {(0, 2): 0, (0, 3): 1, (1, 2): 2, (1, 3): 3, (0, 4): 4, (1, 4): 5, (2, 4): 6, (3, 4): 7}
     right = f4 + [probe_halves]
+
+    def later_blocks(p):
+        first = 2 if p < 2 else 4
+        wide = tuple(jnp.concatenate([right[q][h] for q in range(first, 5)], axis=1) for h in range(2))
+        products = dot3(f4[p], wide, TN)
+        for q in range(first, 5):
+            at_block = place[p, q] * COLS
+            part3[at_block : at_block + COLS] = products[:, (q - first) * COLS : (q - first + 1) * COLS]
+
+    sum_now.scatter()
     for p in range(NY_CHIPS):
-        wide = tuple(jnp.concatenate([right[q][h] for q in range(p + 1, 5)], axis=1) for h in range(2))
-        products = dot3(f4[p], wide, TN)
-        for q in range(p + 1, 5):
-            at_block = place[p, q] * COLS
-            part2[at_block : at_block + COLS] = products[:, (q - p - 1) * COLS : (q - p) * COLS]
-    all_sum(part2, gath2, cbuf2, zbuf2, xbuf2, ybuf2)
+        later_blocks(p)
+    sum_later.start()
+    sum_later.scatter()
+    sum_now.along_z()
+    sum_later.along_z()
+    sum_now.gather()
+    sum_later.gather()
+    sum_now.share()
     arrive(diag_came)
+    sum_now.finish()
 
     def summed(index):
-        return gath2[index * COLS : (index + 1) * COLS]
-
-    gram_low = block_2x2(diag[0], summed(0), diag[1])
-    gram_high = block_2x2(diag[2], summed(1), diag[3])
+        return gath3[index * COLS : (index + 1) * COLS]
+
+    gram_low = block_2x2(diag[0], gath2[:COLS], diag[1])
+    gram_high = block_2x2(diag[2], gath2[COLS:], diag[3])
     start_sign(gram_low, sign.at[0])
     start_sign(gram_high, sign.at[1])
-    run_signs(sign.at[0], sign.at[1])
+    run_signs(6, sign.at[0], sign.at[1])
+    sum_later.share()
+    run_signs(SIGN_STEPS - 6, sign.at[0], sign.at[1])
+    sum_later.finish()
     low, high = combine_of(sign.at[0]), combine_of(sign.at[1])
     low_h, high_h = halves(low), halves(high)
     crossing = jnp.concatenate(
-        [jnp.concatenate([summed(2), summed(3)], axis=1), jnp.concatenate([summed(4), summed(5)], axis=1)], axis=0
+        [jnp.concatenate([summed(0), summed(1)], axis=1), jnp.concatenate([summed(2), summed(3)], axis=1)], axis=0
     )
     diag_low = dot3(low_h, halves(dot3(halves(gram_low), low_h)), TN)
     diag_high = dot3(high_h, halves(dot3(halves(gram_high), high_h)), TN)
     cross = dot3(low_h, halves(dot3(halves(crossing), high_h)), TN)
 
     start_sign(block_2x2(diag_low, cross, diag_high), sign.at[0])
-    run_signs(sign.at[0])
+    run_signs(SIGN_STEPS, sign.at[0])
     last = combine_of(sign.at[0])
     whole = halves(
         jnp.concatenate([dot3(low_h, halves(last[:COLS])), dot3(high_h, halves(last[COLS:]))], axis=0)
     )
     all4 = tuple(jnp.concatenate([f[h] for f in [halves(rows4[p]) for p in range(NY_CHIPS)]], axis=1) for h in range(2))
     basis = dot3(all4, whole)
-    turned[...] = basis.T
+    for k in range(own_rows // out_cells):
+        turned[k] = basis[k * out_cells : (k + 1) * out_cells].T
     width = COLS // 8
+
+    def grid_rows(place):
+        count = own_rows // out_cells
+        return pl.ds(place * count, count)
+
     place_own = core * NY_CHIPS + y
     came = []
     for f in range(2):
@@ -349,18 +435,17 @@
                 to_t = ((y + d) % NY_CHIPS) * 2 + (core + f) % 2
                 from_place = ((core + f) % 2) * NY_CHIPS + (y + NY_CHIPS - d) % NY_CHIPS
                 came.append(
-                    push(turned.at[rows_at(to_t * width, width)], pieces.at[place_own], at(d_y=d, flip=f), pieces.at[from_place])
+                    push(
+                        turned.at[:, rows_at(to_t * width, width)], pieces.at[grid_rows(place_own)], at(d_y=d, flip=f),
+                        pieces.at[grid_rows(from_place)],
+                    )
                 )
-    pieces[place_own] = turned[rows_at(t * width, width), :]
-    coef_all[...] = mul_pair(whole, gath2)
+    pieces[grid_rows(place_own)] = turned[:, rows_at(t * width, width), :]
+    coef_all[...] = dot3(whole, halves(gath3[4 * COLS :]), TN)
     coef[...] = coef_all[rows_at(t * width, width), :]
     arrive(came)
     for out in unsent:
         out.wait_send()
-
-
-def mul_pair(whole, gath2):
-    return dot3(whole, halves(gath2[6 * COLS :]), TN)
 
 
 def merge_all(snapshots, mask, taps_rows, taps_cols, probes):
@@ -369,18 +454,19 @@
     half = rows // 2
     own_rows = half // NY_CHIPS
     f32, vmem = jnp.float32, pltpu.VMEM
-    piece1, piece2 = FIRST_ROWS // 16, SECOND_ROWS // 16
+    piece1 = FIRST_ROWS // 2 // NZ_CHIPS
+    piece2, piece3 = SECOND_ROWS // 2 // XY_CHIPS, LATER_ROWS // 2 // XY_CHIPS
     return pl.pallas_call(
         merge_kernel,
         out_shape=(
-            jax.ShapeDtypeStruct((8, cols // 8, own_rows), f32),
+            jax.ShapeDtypeStruct((rows_dev // 2, cols // 8, cells // 2), f32),
             jax.ShapeDtypeStruct((cols // 8, cols), f32),
         ),
-        in_specs=[pl.BlockSpec(memory_space=pl.ANY)] * 2
-        + [pl.BlockSpec(memory_space=pltpu.SMEM)] * 2
-        + [pl.BlockSpec(memory_space=pl.ANY)],
+        in_specs=[pl.BlockSpec(memory_space=pl.ANY)] * 5,
         out_specs=(pl.BlockSpec(memory_space=pltpu.VMEM), pl.BlockSpec(memory_space=pltpu.VMEM)),
         scratch_shapes=[
+            pltpu.SMEM((TAPS,), f32),
+            pltpu.SMEM((TAPS,), f32),
             vmem((rows_dev + 4, cells, cols), f32),
             vmem((COLS, cells), jnp.int32),
             vmem((16, cells), jnp.int32),
@@ -401,20 +487,24 @@
             vmem((SECOND_ROWS, cols), f32),
             vmem((SECOND_ROWS, cols), f32),
             vmem((SECOND_ROWS // 2, cols), f32),
-            vmem((NZ_CHIPS - 1, piece2, cols), f32),
-            vmem((NX_CHIPS, piece2, cols), f32),
-            vmem((NY_CHIPS, piece2, cols), f32),
+            vmem((XY_CHIPS - 1, piece2, cols), f32),
+            vmem((NZ_CHIPS, piece2, cols), f32),
+            vmem((LATER_ROWS, cols), f32),
+            vmem((LATER_ROWS, cols), f32),
+            vmem((LATER_ROWS // 2, cols), f32),
+            vmem((XY_CHIPS - 1, piece3, cols), f32),
+            vmem((NZ_CHIPS, piece3, cols), f32),
             vmem((2, 2 * cols, 2 * cols), f32),
             vmem((own_rows, cols), f32),
-            vmem((cols, own_rows), f32),
+            vmem((own_rows * 2 // cells, cols, cells // 2), f32),
             vmem((cols, cols), f32),
-            pltpu.SemaphoreType.DMA((64,)),
-            pltpu.SemaphoreType.DMA((64,)),
-            pltpu.SemaphoreType.DMA((2,)),
+            pltpu.SemaphoreType.DMA((128,)),
+            pltpu.SemaphoreType.DMA((128,)),
+            pltpu.SemaphoreType.DMA((4,)),
             pltpu.SemaphoreType.DMA((rows_dev // CHUNK,)),
         ],
         compiler_params=pltpu.CompilerParams(
-            collective_id=1, has_side_effects=True, vmem_limit_bytes=32 << 20
+            collective_id=1, has_side_effects=True
         ),
         name="merge_all",
     )(snapshots, mask, taps_rows, taps_cols, probes)
@@ -425,8 +515,7 @@
     cell_rows = rows_dev // 2 * (cell_cols // 2)
     flat_probes = probes.reshape(cell_rows, probes.shape[2])
     pieces, coef_own = merge_all(snapshots, land_mask, taps_rows, taps_cols, flat_probes)
-    basis_own = pieces.transpose(0, 2, 1)
-    return (basis_own.reshape(rows_dev // 2, cell_cols // 2, columns // 8), coef_own)
+    return (pieces.transpose(0, 2, 1), coef_own)
 
 
 def solution(mesh):

time: 106 us -> 93.9 us (0.89)
  Pallas kernels: 97.9 us -> 90.1 us
  local copies, waits for them, and re-layouts: 7.11 us -> 2.96 us
    pallas_call x1, Pallas kernels: 97.9 us -> 90.1 us  [merge_all(): pl.pallas_call(merge_kernel, out_shape=(jax.ShapeDtypeStruct((rows_dev //...]
    unnamed x12 -> x2, local copies, waits for them, and re-layouts: 6.93 us -> 2.96 us
where the time goes in v3:
time: 93.9 us; the launch traced here: 93.7 us
  Pallas kernels  90.1 us (96%)
  local copies, waits for them, and re-layouts  2.96 us (3%)
    pallas_call x1, Pallas kernels, merge_all(): pl.pallas_call(merge_kernel, out_shape=(jax.ShapeDtypeStruct((rows_dev //...  90.1 us
    unnamed x2, local copies, waits for them, and re-layouts  2.96 us

profile of v3, /device:TPU:1, one launch (start us, length us, event | category | flops | bytes accessed | tf_op | source)
XLA Modules:
  0.0 93.7 jit_solution(8675498187217706706)
XLA Ops:
  0.6 90.1 %merge_all.1 = (f32[32,16,64]{2,1,0:T(8,128)}, f32[16,128]{1,0:T(8,128)}) custom-call(f32[64,128,128]{2,1,0:T(8,128)} %snapshots.1, s32[64,128]{1,0:T(8,128)} %mask.1, f32[6]{0:T(128)} %taps_rows.1, f32[6]{0:T(128)} %taps_cols.1, f32[2048,128]{1,0:T(8,128)} %bitcast.2), custom_call_target="tpu_custom_call" | custom-call | tf_op jit(solution)/shard_map/merge_all/pallas_call | solution.py:459
  90.8 1.7 %copy.9 = f32[32,64,16]{1,2,0:T(8,128)} copy(f32[32,64,16]{1,2,0:T(8,128)} %bitcast.3) | data formatting | bytes 262144
  92.5 1.3 %copy.10 = f32[16,128]{1,0:T(8,128)} copy(f32[16,128]{1,0:T(8,128)} %get-tuple-element.9) | data formatting | bytes 16384

commit v4 on v3

v4 whole, which is shorter than its diff:
```python
import functools

import jax
import jax.numpy as jnp
from jax import lax
from jax.experimental import pallas as pl
from jax.experimental.pallas import tpu as pltpu
from jax.sharding import PartitionSpec as P

SIGN_STEPS = 8
GROUPS = 21
NX_CHIPS, NY_CHIPS, NZ_CHIPS = 4, 4, 8
SPACE, XY_CHIPS = NX_CHIPS * NZ_CHIPS, NX_CHIPS * NY_CHIPS
COLS = 128
FIRST_ROWS, SECOND_ROWS, LATER_ROWS = 3 * COLS, 2 * COLS, 8 * COLS
TAPS, CHUNK, EDGE, MARGIN = 6, 8, 8, 4
MESH = pl.DeviceIdType.MESH

def rows_at(start, size):
    return pl.ds(pl.multiple_of(start, 8), size)


NN = (((1,), (0,)), ((), ()))
TN = (((0,), (0,)), ((), ()))


def halves(a):
    high = a.astype(jnp.bfloat16)
    return high, (a - high.astype(jnp.float32)).astype(jnp.bfloat16)


def dot(a, b, dims):
    return lax.dot_general(a, b, dims, preferred_element_type=jnp.float32)


def dot3(a, b, dims=NN):
    (a_high, a_low), (b_high, b_low) = a, b
    (a_dim,), (b_dim,) = dims[0]
    left = jnp.concatenate([a_high, a_low, a_high], axis=a_dim)
    right = jnp.concatenate([b_high, b_high, b_low], axis=b_dim)
    return dot(left, right, dims)


def mul(a, b, dims=NN):
    return dot3(halves(a), halves(b), dims)


def block_2x2(low, cross, high):
    return jnp.concatenate(
        [jnp.concatenate([low, cross], axis=1), jnp.concatenate([cross.T, high], axis=1)], axis=0
    )


def start_sign(gram, y_ref):
    order = gram.shape[0]
    identity = lax.broadcasted_iota(jnp.int32, gram.shape, 0) == lax.broadcasted_iota(jnp.int32, gram.shape, 1)
    mean_eig = jnp.sum(jnp.where(identity, gram, 0.0), keepdims=True) / order
    shifted = gram - jnp.where(identity, mean_eig, 0.0)
    y_ref[...] = shifted / jnp.sqrt(jnp.sum(shifted * shifted, keepdims=True) + 1e-06)


def sign_step(y_ref):
    y = y_ref[...]
    y_halves = halves(y)
    square = dot3(y_halves, y_halves)
    y_ref[...] = 1.5 * y - 0.5 * dot3(y_halves, halves(square))


def combine_of(y_ref):
    y = y_ref[...]
    order = y.shape[0]
    row = lax.broadcasted_iota(jnp.int32, (order, order // 2), 0)
    col = lax.broadcasted_iota(jnp.int32, (order, order // 2), 1)
    ones = jnp.where((row == col) | (row == col + order // 2), 0.5, 0.0)
    return ones + 0.5 * (y[:, : order // 2] + y[:, order // 2 :])


def run_signs(steps, *refs):
    def body(step, carry):
        for ref in refs:
            sign_step(ref)
        return carry

    lax.fori_loop(0, steps, body, 0)


def merge_kernel(snapshots, mask, taps_rows, taps_cols, probes, pieces, coef,
                 row_taps, col_taps, field, mask_own, tall, edges, edge_in, away, pair, cat_high, cat_low, gram, part1, gath1, cbuf1, zbuf1, xbuf1,
                 quarter, rows4, diag, part2, gath2, cbuf2, rbuf2, zbuf2,
                 part3, gath3, cbuf3, rbuf3, zbuf3, sign, probe_rows, turned, coef_all, combines, diag_next,
                 send, recv, local_sem, chunk_sem):
    t = lax.axis_index("tm")
    s = lax.axis_index("space")
    y, core = t // 2, t % 2
    x, z = s // NZ_CHIPS, s % NZ_CHIPS
    rows_dev, cells = snapshots.shape[0], snapshots.shape[1]
    out_rows, out_cells = rows_dev // 2, cells // 2
    half = out_rows * out_cells // 2
    chunks = rows_dev // CHUNK
    own_rows = half // NY_CHIPS

    def at(d_z=0, d_x=0, d_y=0, flip=0):
        c = (core + flip) % 2
        return {
            "tm": ((y + d_y) % NY_CHIPS) * 2 + c,
            "space": ((x + d_x) % NX_CHIPS) * NZ_CHIPS + (z + d_z) % NZ_CHIPS,
        }

    z_offsets = range(1, NZ_CHIPS)
    x_offsets = range(1, NX_CHIPS)
    y_offsets = range(1, NY_CHIPS)
    s_above, s_below = (s + SPACE - 1) % SPACE, (s + 1) % SPACE
    barrier = pltpu.get_barrier_semaphore()
    xy_offsets = [(a, b) for a in range(NX_CHIPS) for b in range(NY_CHIPS) if a or b]
    peers = [at(d_z=d) for d in z_offsets] + [at(d_x=a, d_y=b) for a, b in xy_offsets]
    peers += [at(d_y=d, flip=1) for d in range(NY_CHIPS)]
    peers += [{"tm": 2 * y + c, "space": there} for c in range(2) for there in (s_above, s_below)]
    for peer in peers:
        pl.semaphore_signal(barrier, inc=1, device_id=peer, device_id_type=MESH)

    count = [0]
    unsent = []

    class Group:
        def __init__(self, landed):
            self.index, self.landed = count[0], landed
            count[0] += 1
            unsent.append(self)

        def make(self, src, dst, to):
            return pltpu.make_async_remote_copy(
                src_ref=src, dst_ref=dst, send_sem=send.at[self.index], recv_sem=recv.at[self.index],
                device_id=to, device_id_type=MESH,
            )

        def push(self, src, dst, to):
            self.make(src, dst, to).start()
            return self

        def arrive(self):
            self.make(self.landed, self.landed, at(flip=1)).wait_recv()

        def wait_send(self):
            self.make(self.landed, self.landed, at(flip=1)).wait_send()

    def push(src, dst, to, landed):
        return Group(landed).push(src, dst, to)

    take_probes = pltpu.make_async_copy(
        probes.at[rows_at(core * half + y * own_rows, own_rows)], probe_rows, local_sem.at[0]
    )
    take_probes.start()
    take_mask = pltpu.make_async_copy(mask, mask_own.at[pl.ds(0, rows_dev)], local_sem.at[1])
    take_mask.start()
    take_taps = [
        pltpu.make_async_copy(taps_rows, row_taps, local_sem.at[2]),
        pltpu.make_async_copy(taps_cols, col_taps, local_sem.at[3]),
    ]
    for taps in take_taps:
        taps.start()

    order = [0, chunks - 1] + list(range(1, chunks - 1))

    def chunk_first(k):
        return (core * k + (1 - core) * (chunks - 1 - k)) * CHUNK

    def chunk_copy(k):
        first = chunk_first(k)
        return pltpu.make_async_copy(
            snapshots.at[pl.ds(first, CHUNK)], field.at[pl.ds(first + MARGIN, CHUNK)], chunk_sem.at[k]
        )

    for k in order:
        chunk_copy(k).start()
    for margin in (0, MARGIN + rows_dev):
        field[pl.ds(margin, MARGIN)] = jnp.zeros((MARGIN, cells, COLS), jnp.float32)
    mask_own[rows_dev:, :] = jnp.zeros((COLS - rows_dev, cells), jnp.int32)
    tall[:, :EDGE] = jnp.zeros((tall.shape[0], EDGE, COLS), jnp.float32)
    tall[:, EDGE + cells :] = jnp.zeros((tall.shape[0], EDGE, COLS), jnp.float32)
    take_mask.wait()
    mask_cols = mask_own[...].astype(jnp.float32).T

    def mask_chunk(k):
        chunk_copy(k).wait()
        first = chunk_first(k)
        turned_mask = pltpu.roll(mask_cols, (COLS - first) % COLS, axis=1)
        for r in range(CHUNK):
            field[first + MARGIN + r] = field[first + MARGIN + r] * turned_mask[:, r : r + 1]

    for taps in take_taps:
        taps.wait()
    tr = [row_taps[k] for k in range(TAPS)]
    tc = [col_taps[k] for k in range(TAPS)]

    def filter_row(i, slot):
        total = tr[0] * field[2 * i + MARGIN - 2]
        for k in range(1, TAPS):
            total = total + tr[k] * field[2 * i + MARGIN - 2 + k]
        tall[slot, EDGE : EDGE + cells] = total
        out = tc[0] * tall[slot, pl.ds(EDGE - 2, out_cells, stride=2), :]
        for k in range(1, TAPS):
            out = out + tc[k] * tall[slot, pl.ds(EDGE - 2 + k, out_cells, stride=2), :]
        return out

    def filter_half(which, store):
        slots = tall.shape[0]

        def body(step, carry):
            for slot in range(slots):
                n = step * slots + slot
                store(rows_at(n * out_cells, out_cells), filter_row(which * (out_rows // 2) + n, slot))
            return carry

        lax.fori_loop(0, out_rows // 2 // slots, body, 0)

    def store_away(rows, value):
        away[rows, :] = value

    def store_own(rows, value):
        pair[core, rows, :] = value

    for k in order[:2]:
        mask_chunk(k)
    edges[0] = filter_row(-1, 0)
    edges[1] = filter_row(out_rows, 1)
    for k in order[2 : chunks // 2 + 2]:
        mask_chunk(k)
    filter_half(1 - core, store_away)
    pl.semaphore_wait(barrier, len(peers))
    crossed = push(away, pair.at[core], at(flip=1), pair.at[1 - core])
    edge_group = Group(edge_in)
    edge_group.push(edges.at[0], edge_in.at[core], {"tm": 2 * y + 1, "space": s_above})
    edge_group.push(edges.at[1], edge_in.at[core], {"tm": 2 * y, "space": s_below})
    for k in order[chunks // 2 + 2 :]:
        mask_chunk(k)
    filter_half(core, store_own)
    edge_group.arrive()
    crossed.arrive()
    touches = ((s > 0) & (core == 0)) | ((s < SPACE - 1) & (core == 1))
    edge_rows = rows_at((out_rows // 2 - 1) * out_cells * core, out_cells)
    for c in range(2):
        pair[c, edge_rows, :] = pair[c, edge_rows, :] + jnp.where(touches, edge_in[c], 0.0)

    def plane_sum(part, gath, cbuf, zbuf, xbuf):
        rows = part.shape[0] // 2
        piece = rows // NZ_CHIPS
        mine = core * rows
        push(part.at[rows_at((1 - core) * rows, rows)], cbuf, at(flip=1), cbuf).arrive()
        part[rows_at(mine, rows), :] = part[rows_at(mine, rows), :] + cbuf[...]
        group = Group(zbuf)
        for d in z_offsets:
            group.push(part.at[rows_at(mine + (z + d) % NZ_CHIPS * piece, piece)], zbuf.at[d - 1], at(d_z=d))
        group.arrive()
        total = part[rows_at(mine + z * piece, piece), :]
        for d in z_offsets:
            total = total + zbuf[d - 1]
        xbuf[x] = total
        group = Group(xbuf.at[pl.ds(0, NX_CHIPS - 1)])
        for d in x_offsets:
            group.push(xbuf.at[x], xbuf.at[x], at(d_x=d))
        group.arrive()
        own = gath.at[rows_at(mine + z * piece, piece)]
        gath[rows_at(mine + z * piece, piece), :] = (xbuf[0] + xbuf[1]) + (xbuf[2] + xbuf[3])
        group = Group(gath.at[rows_at(mine, (NZ_CHIPS - 1) * piece)])
        for d in z_offsets:
            group.push(own, own, at(d_z=d))
        group.arrive()
        ours, theirs = gath.at[rows_at(mine, rows)], gath.at[rows_at((1 - core) * rows, rows)]
        push(ours, ours, at(flip=1), theirs).arrive()

    class WholeSum:
        def __init__(self, part, gath, cbuf, rbuf, zbuf):
            self.part, self.gath, self.cbuf, self.rbuf, self.zbuf = part, gath, cbuf, rbuf, zbuf
            self.rows = part.shape[0] // 2
            self.piece = self.rows // XY_CHIPS
            self.ours = rows_at(core * self.rows, self.rows)
            self.theirs = rows_at((1 - core) * self.rows, self.rows)

        def piece_of(self, a, b):
            owner = (x + a) % NX_CHIPS * NY_CHIPS + (y + b) % NY_CHIPS
            return rows_at(core * self.rows + owner * self.piece, self.piece)

        def start(self):
            self.came = push(self.part.at[self.theirs], self.cbuf, at(flip=1), self.cbuf)

        def scatter(self):
            self.came.arrive()
            self.part[self.ours, :] = self.part[self.ours, :] + self.cbuf[...]
            self.came = Group(self.rbuf)
            for n, (a, b) in enumerate(xy_offsets):
                self.came.push(self.part.at[self.piece_of(a, b)], self.rbuf.at[n], at(d_x=a, d_y=b))

        def along_z(self):
            self.came.arrive()
            total = self.part[self.piece_of(0, 0), :]
            for n in range(len(xy_offsets)):
                total = total + self.rbuf[n]
            self.zbuf[z] = total
            self.came = Group(self.zbuf.at[pl.ds(0, NZ_CHIPS - 1)])
            for d in z_offsets:
                self.came.push(self.zbuf.at[z], self.zbuf.at[z], at(d_z=d))

        def gather(self):
            self.came.arrive()
            terms = [self.zbuf[k] for k in range(NZ_CHIPS)]
            while len(terms) > 1:
                terms = [terms[k] + terms[k + 1] for k in range(0, len(terms), 2)]
            own = self.piece_of(0, 0)
            self.gath[own, :] = terms[0]
            own = self.gath.at[own]
            self.came = Group(self.gath.at[rows_at(core * self.rows, (XY_CHIPS - 1) * self.piece)])
            for a, b in xy_offsets:
                self.came.push(own, own, at(d_x=a, d_y=b))

        def share(self):
            self.came.arrive()
            ours, theirs = self.gath.at[self.ours], self.gath.at[self.theirs]
            self.came = push(ours, ours, at(flip=1), theirs)

        def finish(self):
            self.came.arrive()

    gram[...] = jnp.zeros_like(gram)

    def add_rows(chunk, carry):
        rows = rows_at(chunk * own_rows, own_rows)
        high, low = halves(jnp.concatenate([pair[0, rows, :], pair[1, rows, :]], axis=1))
        cat_high[rows, :] = high
        cat_low[rows, :] = low
        cross = dot(high, low, TN)
        gram[...] = gram[...] + (dot(high, high, TN) + (cross + cross.T))
        return carry

    lax.fori_loop(0, NY_CHIPS, add_rows, 0)
    part1[:COLS] = gram[:COLS, :COLS]
    part1[COLS : 2 * COLS] = gram[:COLS, COLS:]
    part1[2 * COLS :] = gram[COLS:, COLS:]
    plane_sum(part1, gath1, cbuf1, zbuf1, xbuf1)
    total = block_2x2(gath1[:COLS], gath1[COLS : 2 * COLS], gath1[2 * COLS :])
    start_sign(total, sign.at[0])
    run_signs(SIGN_STEPS, sign.at[0])
    combine = combine_of(sign.at[0])
    combine_halves = halves(combine)

    quarters = Group(rows4.at[pl.ds(0, NY_CHIPS - 1)])
    for d in [2, 1, 3, 0]:
        to = (y + d) % NY_CHIPS
        rows = rows_at(to * own_rows, own_rows)
        merged = dot3((cat_high[rows, :], cat_low[rows, :]), combine_halves)
        if d:
            quarter[d - 1] = merged
            quarters.push(quarter.at[d - 1], rows4.at[y], at(d_y=d))
        else:
            rows4[y] = merged
    diag[y] = mul(combine, mul(total, combine), TN)
    diags = Group(diag.at[pl.ds(0, NY_CHIPS - 1)])
    for d in y_offsets:
        diags.push(diag.at[y], diag.at[y], at(d_y=d))
    take_probes.wait()
    quarters.arrive()

    f4 = [halves(rows4[p]) for p in range(NY_CHIPS)]
    probe_halves = halves(probe_rows[...])
    sum_now = WholeSum(part2, gath2, cbuf2, rbuf2, zbuf2)
    sum_later = WholeSum(part3, gath3, cbuf3, rbuf3, zbuf3)

    def beside(*blocks):
        return tuple(jnp.concatenate([block[h] for block in blocks], axis=1) for h in range(2))

    products = dot3(beside(f4[0], f4[2]), beside(f4[1], f4[3]), TN)
    part2[:COLS] = products[:COLS, :COLS]
    part2[COLS:] = products[COLS:, COLS:]
    sum_now.start()
    sum_now.scatter()
    products = dot3(beside(f4[0], f4[1]), beside(f4[2], f4[3], probe_halves), TN)
    for n, (p, q) in enumerate([(0, 0), (0, 1), (1, 0), (1, 1), (0, 2), (1, 2)]):
        part3[n * COLS : (n + 1) * COLS] = products[p * COLS : (p + 1) * COLS, q * COLS : (q + 1) * COLS]
    part3[6 * COLS :] = dot3(beside(f4[2], f4[3]), probe_halves, TN)
    sum_later.start()
    sum_later.scatter()
    sum_now.along_z()
    sum_later.along_z()
    sum_now.gather()
    sum_later.gather()
    sum_now.share()
    diags.arrive()
    sum_now.finish()

    def summed(index):
        return gath3[index * COLS : (index + 1) * COLS]

    def gram_of(which):
        return block_2x2(diag[2 * which], gath2[rows_at(which * COLS, COLS), :], diag[2 * which + 1])

    def diag_of(which):
        c = halves(combines[which])
        return dot3(c, halves(dot3(halves(gram_of(which)), c)), TN)

    start_sign(gram_of(core), sign.at[0])
    run_signs(6, sign.at[0])
    sum_later.share()
    run_signs(SIGN_STEPS - 6, sign.at[0])
    combines[core] = combine_of(sign.at[0])
    swapped = push(combines.at[core], combines.at[core], at(flip=1), combines.at[1 - core])
    diag_next[core] = diag_of(core)
    sum_later.finish()
    swapped.arrive()
    diag_next[1 - core] = diag_of(1 - core)
    low_h, high_h = halves(combines[0]), halves(combines[1])
    crossing = jnp.concatenate(
        [jnp.concatenate([summed(0), summed(1)], axis=1), jnp.concatenate([summed(2), summed(3)], axis=1)], axis=0
    )
    cross = dot3(low_h, halves(dot3(halves(crossing), high_h)), TN)

    start_sign(block_2x2(diag_next[0], cross, diag_next[1]), sign.at[0])
    run_signs(SIGN_STEPS, sign.at[0])
    last = combine_of(sign.at[0])
    whole = halves(
        jnp.concatenate([dot3(low_h, halves(last[:COLS])), dot3(high_h, halves(last[COLS:]))], axis=0)
    )
    all4 = tuple(jnp.concatenate([f[h] for f in [halves(rows4[p]) for p in range(NY_CHIPS)]], axis=1) for h in range(2))
    basis = dot3(all4, whole)
    for k in range(own_rows // out_cells):
        turned[k] = basis[k * out_cells : (k + 1) * out_cells].T
    width = COLS // 8

    def grid_rows(place):
        count = own_rows // out_cells
        return pl.ds(place * count, count)

    place_own = core * NY_CHIPS + y
    outward = Group(pieces.at[pl.ds(0, out_rows - out_rows // 8)])
    for f in range(2):
        for d in range(NY_CHIPS):
            if d or f:
                to_t = ((y + d) % NY_CHIPS) * 2 + (core + f) % 2
                outward.push(
                    turned.at[:, rows_at(to_t * width, width)], pieces.at[grid_rows(place_own)], at(d_y=d, flip=f)
                )
    pieces[grid_rows(place_own)] = turned[:, rows_at(t * width, width), :]
    coef_all[...] = dot3(whole, halves(gath3[4 * COLS :]), TN)
    coef[...] = coef_all[rows_at(t * width, width), :]
    outward.arrive()
    assert count[0] == GROUPS
    for out in unsent:
        out.wait_send()


def merge_all(snapshots, mask, taps_rows, taps_cols, probes):
    rows_dev, cells, cols = snapshots.shape
    rows = rows_dev // 2 * (cells // 2)
    half = rows // 2
    own_rows = half // NY_CHIPS
    f32, vmem = jnp.float32, pltpu.VMEM
    piece1 = FIRST_ROWS // 2 // NZ_CHIPS
    piece2, piece3 = SECOND_ROWS // 2 // XY_CHIPS, LATER_ROWS // 2 // XY_CHIPS
    return pl.pallas_call(
        merge_kernel,
        out_shape=(
            pltpu.VMEM((rows_dev // 2, cols // 8, cells // 2), f32),
            pltpu.VMEM((cols // 8, cols), f32),
        ),
        in_specs=[pl.BlockSpec(memory_space=pl.ANY)] * 5,
        out_specs=(pl.BlockSpec(memory_space=pltpu.VMEM), pl.BlockSpec(memory_space=pltpu.VMEM)),
        scratch_shapes=[
            pltpu.SMEM((TAPS,), f32),
            pltpu.SMEM((TAPS,), f32),
            vmem((rows_dev + 2 * MARGIN, cells, cols), f32),
            vmem((COLS, cells), jnp.int32),
            vmem((4, cells + 2 * EDGE, cols), f32),
            vmem((2, cells // 2, cols), f32),
            vmem((2, cells // 2, cols), f32),
            vmem((half, cols), f32),
            vmem((2, half, cols), f32),
            vmem((half, 2 * cols), jnp.bfloat16),
            vmem((half, 2 * cols), jnp.bfloat16),
            vmem((2 * cols, 2 * cols), f32),
            vmem((FIRST_ROWS, cols), f32),
            vmem((FIRST_ROWS, cols), f32),
            vmem((FIRST_ROWS // 2, cols), f32),
            vmem((NZ_CHIPS - 1, piece1, cols), f32),
            vmem((NX_CHIPS, piece1, cols), f32),
            vmem((NY_CHIPS - 1, own_rows, cols), f32),
            vmem((NY_CHIPS, own_rows, cols), f32),
            vmem((NY_CHIPS, cols, cols), f32),
            vmem((SECOND_ROWS, cols), f32),
            vmem((SECOND_ROWS, cols), f32),
            vmem((SECOND_ROWS // 2, cols), f32),
            vmem((XY_CHIPS - 1, piece2, cols), f32),
            vmem((NZ_CHIPS, piece2, cols), f32),
            vmem((LATER_ROWS, cols), f32),
            vmem((LATER_ROWS, cols), f32),
            vmem((LATER_ROWS // 2, cols), f32),
            vmem((XY_CHIPS - 1, piece3, cols), f32),
            vmem((NZ_CHIPS, piece3, cols), f32),
            vmem((1, 2 * cols, 2 * cols), f32),
            vmem((own_rows, cols), f32),
            vmem((own_rows * 2 // cells, cols, cells // 2), f32),
            vmem((cols, cols), f32),
            vmem((2, 2 * cols, cols), f32),
            vmem((2, cols, cols), f32),
            pltpu.SemaphoreType.DMA((GROUPS,)),
            pltpu.SemaphoreType.DMA((GROUPS,)),
            pltpu.SemaphoreType.DMA((4,)),
            pltpu.SemaphoreType.DMA((rows_dev // CHUNK,)),
        ],
        compiler_params=pltpu.CompilerParams(
            collective_id=1, has_side_effects=True
        ),
        name="merge_all",
    )(snapshots, mask, taps_rows, taps_cols, probes)


def local(snapshots, land_mask, taps_rows, taps_cols, probes):
    rows_dev, cell_cols, columns = snapshots.shape
    cell_rows = rows_dev // 2 * (cell_cols // 2)
    flat_probes = probes.reshape(cell_rows, probes.shape[2])
    pieces, coef_own = merge_all(snapshots, land_mask, taps_rows, taps_cols, flat_probes)
    return (pieces.transpose(0, 2, 1), coef_own)


def solution(mesh):
    placed = (P("space", None, "tm"), P("space", None), P(), P(), P("space", None, None))
    return jax.shard_map(
        local,
        mesh=mesh,
        in_specs=placed,
        out_specs=(P("space", None, "tm"), P("tm", None)),
        check_vma=False,
    )
```

time: 93.9 us -> 87.5 us (0.932)
  Pallas kernels: 90.1 us -> 85.5 us
  local copies, waits for them, and re-layouts: 2.96 us -> 1.3 us
    pallas_call x1, Pallas kernels: 90.1 us -> 85.5 us  [merge_all(): pl.pallas_call(merge_kernel, out_shape=(pltpu.VMEM((rows_dev // 2, cols /...]
    unnamed x2, local copies, waits for them, and re-layouts: 2.96 us -> 1.3 us
where the time goes in v4:
time: 87.5 us; the launch traced here: 87.4 us
  Pallas kernels  85.5 us (98%)
  local copies, waits for them, and re-layouts  1.3 us (1%)
    pallas_call x1, Pallas kernels, merge_all(): pl.pallas_call(merge_kernel, out_shape=(pltpu.VMEM((rows_dev // 2, cols /...  85.5 us

profile of v4, /device:TPU:1, one launch (start us, length us, event | category | flops | bytes accessed | tf_op | source)
XLA Modules:
  0.0 87.4 jit_solution(370524783424546441)
XLA Ops:
  0.6 85.5 %merge_all.1 = (f32[32,16,64]{2,1,0:T(8,128)S(1)}, f32[16,128]{1,0:T(8,128)S(1)}) custom-call(f32[64,128,128]{2,1,0:T(8,128)} %snapshots.1, s32[64,128]{1,0:T(8,128)} %mask.1, f32[6]{0:T(128)} %taps_rows.1, f32[6]{0:T(128)} %taps_cols.1, f32[2048,128]{1,0:T(8,128)} %bitcast.3), custom_call_target="tpu_custom_call" | custom-call | tf_op jit(solution)/shard_map/merge_all/pallas_call | solution.py:457
  86.1 0.7 copy.9
  86.8 0.6 copy.10

commit v5 on v4

--- a/solution.py
+++ b/solution.py
@@ -99,6 +99,24 @@
     chunks = rows_dev // CHUNK
     own_rows = half // NY_CHIPS
 
+    take_mask = pltpu.make_async_copy(mask, mask_own.at[pl.ds(0, rows_dev)], local_sem.at[1])
+    take_mask.start()
+    take_taps = [
+        pltpu.make_async_copy(taps_rows, row_taps, local_sem.at[2]),
+        pltpu.make_async_copy(taps_cols, col_taps, local_sem.at[3]),
+    ]
+    for taps in take_taps:
+        taps.start()
+
+    chunk_copies = [
+        pltpu.make_async_copy(
+            snapshots.at[pl.ds(k * CHUNK, CHUNK)], field.at[pl.ds(MARGIN + k * CHUNK, CHUNK)], chunk_sem.at[k]
+        )
+        for k in range(chunks)
+    ]
+    for copy in chunk_copies:
+        copy.start()
+
     def at(d_z=0, d_x=0, d_y=0, flip=0):
         c = (core + flip) % 2
         return {
@@ -150,42 +168,18 @@
         probes.at[rows_at(core * half + y * own_rows, own_rows)], probe_rows, local_sem.at[0]
     )
     take_probes.start()
-    take_mask = pltpu.make_async_copy(mask, mask_own.at[pl.ds(0, rows_dev)], local_sem.at[1])
-    take_mask.start()
-    take_taps = [
-        pltpu.make_async_copy(taps_rows, row_taps, local_sem.at[2]),
-        pltpu.make_async_copy(taps_cols, col_taps, local_sem.at[3]),
-    ]
-    for taps in take_taps:
-        taps.start()
-
-    order = [0, chunks - 1] + list(range(1, chunks - 1))
-
-    def chunk_first(k):
-        return (core * k + (1 - core) * (chunks - 1 - k)) * CHUNK
-
-    def chunk_copy(k):
-        first = chunk_first(k)
-        return pltpu.make_async_copy(
-            snapshots.at[pl.ds(first, CHUNK)], field.at[pl.ds(first + MARGIN, CHUNK)], chunk_sem.at[k]
-        )
-
-    for k in order:
-        chunk_copy(k).start()
     for margin in (0, MARGIN + rows_dev):
         field[pl.ds(margin, MARGIN)] = jnp.zeros((MARGIN, cells, COLS), jnp.float32)
     mask_own[rows_dev:, :] = jnp.zeros((COLS - rows_dev, cells), jnp.int32)
     tall[:, :EDGE] = jnp.zeros((tall.shape[0], EDGE, COLS), jnp.float32)
     tall[:, EDGE + cells :] = jnp.zeros((tall.shape[0], EDGE, COLS), jnp.float32)
     take_mask.wait()
-    mask_cols = mask_own[...].astype(jnp.float32).T
+    mask_cols = mask_own[...].astype(jnp.float32).T.astype(jnp.bfloat16)
 
     def mask_chunk(k):
-        chunk_copy(k).wait()
-        first = chunk_first(k)
-        turned_mask = pltpu.roll(mask_cols, (COLS - first) % COLS, axis=1)
-        for r in range(CHUNK):
-            field[first + MARGIN + r] = field[first + MARGIN + r] * turned_mask[:, r : r + 1]
+        for r in range(k * CHUNK, (k + 1) * CHUNK):
+            wet = jnp.broadcast_to(mask_cols[:, r : r + 1], (cells, COLS)).astype(jnp.float32)
+            field[MARGIN + r] = field[MARGIN + r] * wet
 
     for taps in take_taps:
         taps.wait()
@@ -219,20 +213,18 @@
     def store_own(rows, value):
         pair[core, rows, :] = value
 
-    for k in order[:2]:
+    for copy in chunk_copies:
+        copy.wait()
+    for k in range(chunks):
         mask_chunk(k)
     edges[0] = filter_row(-1, 0)
     edges[1] = filter_row(out_rows, 1)
-    for k in order[2 : chunks // 2 + 2]:
-        mask_chunk(k)
     filter_half(1 - core, store_away)
     pl.semaphore_wait(barrier, len(peers))
     crossed = push(away, pair.at[core], at(flip=1), pair.at[1 - core])
     edge_group = Group(edge_in)
     edge_group.push(edges.at[0], edge_in.at[core], {"tm": 2 * y + 1, "space": s_above})
     edge_group.push(edges.at[1], edge_in.at[core], {"tm": 2 * y, "space": s_below})
-    for k in order[chunks // 2 + 2 :]:
-        mask_chunk(k)
     filter_half(core, store_own)
     edge_group.arrive()
     crossed.arrive()

time: 87.5 us -> 85.8 us (0.981)
  Pallas kernels: 85.5 us -> 83.8 us
    pallas_call x1, Pallas kernels: 85.5 us -> 83.8 us  [merge_all(): pl.pallas_call(merge_kernel, out_shape=(pltpu.VMEM((rows_dev // 2, cols /...]
where the time goes in v5:
time: 85.8 us; the launch traced here: 85.7 us
  Pallas kernels  83.8 us (98%)
  local copies, waits for them, and re-layouts  1.3 us (2%)
    pallas_call x1, Pallas kernels, merge_all(): pl.pallas_call(merge_kernel, out_shape=(pltpu.VMEM((rows_dev // 2, cols /...  83.8 us

profile of v5, /device:TPU:1, one launch (start us, length us, event | category | flops | bytes accessed | tf_op | source)
XLA Modules:
  0.0 85.7 jit_solution(15815144132545017569)
XLA Ops:
  0.6 83.8 %merge_all.1 = (f32[32,16,64]{2,1,0:T(8,128)S(1)}, f32[16,128]{1,0:T(8,128)S(1)}) custom-call(f32[64,128,128]{2,1,0:T(8,128)} %snapshots.1, s32[64,128]{1,0:T(8,128)} %mask.1, f32[6]{0:T(128)} %taps_rows.1, f32[6]{0:T(128)} %taps_cols.1, f32[2048,128]{1,0:T(8,128)} %bitcast.3), custom_call_target="tpu_custom_call" | custom-call | tf_op jit(solution)/shard_map/merge_all/pallas_call | solution.py:449
  84.4 0.7 copy.9
  85.1 0.6 copy.10

commit v6 on v5

--- a/solution.py
+++ b/solution.py
@@ -63,7 +63,8 @@
     y = y_ref[...]
     y_halves = halves(y)
     square = dot3(y_halves, y_halves)
-    y_ref[...] = 1.5 * y - 0.5 * dot3(y_halves, halves(square))
+    identity = lax.broadcasted_iota(jnp.int32, y.shape, 0) == lax.broadcasted_iota(jnp.int32, y.shape, 1)
+    y_ref[...] = dot3(y_halves, halves(jnp.where(identity, 1.5, 0.0) - 0.5 * square))
 
 
 def combine_of(y_ref):
@@ -81,7 +82,7 @@
             sign_step(ref)
         return carry
 
-    lax.fori_loop(0, steps, body, 0)
+    lax.fori_loop(0, steps, body, 0, unroll=2)
 
 
 def merge_kernel(snapshots, mask, taps_rows, taps_cols, probes, pieces, coef,
@@ -410,7 +411,7 @@
     whole = halves(
         jnp.concatenate([dot3(low_h, halves(last[:COLS])), dot3(high_h, halves(last[COLS:]))], axis=0)
     )
-    all4 = tuple(jnp.concatenate([f[h] for f in [halves(rows4[p]) for p in range(NY_CHIPS)]], axis=1) for h in range(2))
+    all4 = beside(*f4)
     basis = dot3(all4, whole)
     for k in range(own_rows // out_cells):
         turned[k] = basis[k * out_cells : (k + 1) * out_cells].T

time: 85.8 us -> 85.5 us (level)
  no operation moved by 1% of the time
where the time goes in v6:
time: 85.5 us; the launch traced here: 85.4 us
  Pallas kernels  83.5 us (98%)
  local copies, waits for them, and re-layouts  1.3 us (2%)
    pallas_call x1, Pallas kernels, merge_all(): pl.pallas_call(merge_kernel, out_shape=(pltpu.VMEM((rows_dev // 2, cols /...  83.5 us

profile of v6, /device:TPU:1, one launch (start us, length us, event | category | flops | bytes accessed | tf_op | source)
XLA Modules:
  0.0 85.4 jit_solution(12997601038384735641)
XLA Ops:
  0.6 83.5 %merge_all.1 = (f32[32,16,64]{2,1,0:T(8,128)S(1)}, f32[16,128]{1,0:T(8,128)S(1)}) custom-call(f32[64,128,128]{2,1,0:T(8,128)} %snapshots.1, s32[64,128]{1,0:T(8,128)} %mask.1, f32[6]{0:T(128)} %taps_rows.1, f32[6]{0:T(128)} %taps_cols.1, f32[2048,128]{1,0:T(8,128)} %bitcast.3), custom_call_target="tpu_custom_call" | custom-call | tf_op jit(solution)/shard_map/merge_all/pallas_call | solution.py:450
  84.1 0.7 copy.9
  84.8 0.6 copy.10
